TPU v7x, 512 devices: a whole 4x8x8 slice. The times are simulated.
512 devices in a mesh: ta: 8 (over y), gz: 8 (over x, core), xy: 8 (over z).
Axes of the slice: x: 4, y: 8, z: 8, core: 2. Of those that a mesh axis runs over, the one named last changes fastest.
Arguments:
- right_side: float32 [8, 8, 8, 2, 32, 128], P('ta', 'gz', 'xy'), may hold values from -40 to 40
- stencil: float32 [8, 8, 8, 2, 9, 128, 128], P('ta', 'gz', 'xy'), may hold values from -0.5 to 1.5, as said below
- restrict: float32 [8, 8, 8, 2, 32, 128], P('ta', 'gz', 'xy'), may hold values from -0.5 to 0.5
- aggregate: int32 [8, 8, 8, 2], P('ta', 'gz', 'xy'), may hold values from 0 to 63, as said below
- coarsest_inverse: float32 [2048, 2048], P('xy'), may hold values from -0.125 to 0.125
Outputs:
- solution: float32 [8, 8, 8, 2, 32, 128], P('ta', 'gz', 'xy')
- residual: float32 [8, 8, 8, 2, 32, 128], P('ta', 'gz', 'xy')
Inputs may be any that keep to these rules, and one draw needn't show every extreme that they name: `aggregate`: sites are grouped into 2 x 2 x 2 x 2 blocks aligned at even coordinates; each block forms one coarsest site, and the coarsest sites are numbered in an order drawn from the seed. `stencil`: each self block is close to the identity; the other blocks are small and full.
All inputs are finite; a program needn't handle non-finite values.
Results may differ from a plain program's by a relative error of at most 0.0001.
Values sent between devices are 32-bit elements; how exact they have to be, the bound alone decides.
No kernel may reach another device: no remote copies, remote signals or barrier semaphores. Data moves between devices by JAX's collectives and lax.ppermute only.
A program may use at most 64 MiB of HBM per device.

v0:
```python
import jax
import jax.numpy as jnp
from jax import lax
from jax.sharding import PartitionSpec as P


def extended(cells, sides, width):
    for axis, dim in sides:
        count = lax.axis_size(axis)
        head = lax.slice_in_dim(cells, 0, width, axis=dim)
        tail = lax.slice_in_dim(cells, cells.shape[dim] - width, cells.shape[dim], axis=dim)
        cells = jnp.concatenate(
            [
                lax.ppermute(tail, axis, [(i, (i + 1) % count) for i in range(count)]),
                cells,
                lax.ppermute(head, axis, [((i + 1) % count, i) for i in range(count)]),
            ],
            axis=dim,
        )
    return cells


def apply_operator(field, stencil):
    padded = extended(field, (("ta", 0), ("gz", 1), ("xy", 2)), 1)
    centre = field[0, 0, 0]
    stacked = jnp.stack(
        [
            centre,
            padded[2, 1, 1],
            padded[0, 1, 1],
            padded[1, 2, 1],
            padded[1, 0, 1],
            padded[1, 1, 2],
            padded[1, 1, 0],
            jnp.roll(centre, -1, 0),
            jnp.roll(centre, 1, 0),
        ],
        axis=1,
    )
    result = jnp.einsum(
        "xkij,xkrj->xri", stencil[0, 0, 0], stacked, precision=lax.Precision.HIGHEST
    )
    return result[None, None, None]


def inner_sum(one_side, other_side):
    return jnp.sum(one_side * other_side, axis=(0, 1, 2, 3, 5))


def body(right_side, stencil, restrict, aggregate, coarsest_inverse):
    image_first = apply_operator(right_side, stencil)
    cross_first, square_first = lax.psum(
        (inner_sum(image_first, right_side), inner_sum(image_first, image_first)),
        ("ta", "gz", "xy"),
    )
    step_first = cross_first / square_first
    resid_mid = right_side - step_first[:, None] * image_first
    image_raw = apply_operator(resid_mid, stencil)
    correlation_sum = lax.psum(inner_sum(image_first, image_raw), ("ta", "gz", "xy"))
    beta = correlation_sum / square_first
    image_second = image_raw - beta[:, None] * image_first
    direction = resid_mid - beta[:, None] * right_side
    cross_second, square_second = lax.psum(
        (inner_sum(image_second, resid_mid), inner_sum(image_second, image_second)),
        ("ta", "gz", "xy"),
    )
    step_second = cross_second / square_second
    solution_gcr = step_first[:, None] * right_side + step_second[:, None] * direction
    residual = resid_mid - step_second[:, None] * image_second
    vectors = restrict[0, 0, 0]
    comps = vectors.shape[1]
    aggregates = coarsest_inverse.shape[1] // comps
    nrhs_count = residual.shape[4]
    restricted = jnp.einsum(
        "xkc,xrc->xrk", vectors, residual[0, 0, 0], precision=lax.Precision.HIGHEST
    )
    labels = aggregate[0, 0, 0]
    onehot = (labels[:, None] == jnp.arange(aggregates, dtype=jnp.int32)[None, :]).astype(
        jnp.float32
    )
    partial_rhs = jnp.einsum("xa,xrk->akr", onehot, restricted, precision=lax.Precision.HIGHEST)
    partial_rhs = partial_rhs.reshape(aggregates * comps, nrhs_count)
    coarse_rhs = lax.psum(partial_rhs, ("ta", "gz", "xy"))
    rows_part = jnp.dot(
        coarsest_inverse,
        coarse_rhs,
        precision=lax.Precision.HIGHEST,
        preferred_element_type=jnp.float32,
    )
    correction = lax.all_gather(rows_part, "xy", axis=0, tiled=True)
    correction = correction.reshape(aggregates, comps, nrhs_count)
    per_site = jnp.einsum("xa,akr->xkr", onehot, correction, precision=lax.Precision.HIGHEST)
    lifted = jnp.einsum("xkc,xkr->xrc", vectors, per_site, precision=lax.Precision.HIGHEST)
    solution = solution_gcr + lifted[None, None, None]
    return (solution, residual)


def solution(mesh):
    return jax.shard_map(
        body,
        mesh=mesh,
        in_specs=(
            P("ta", "gz", "xy", None, None, None),
            P("ta", "gz", "xy", None, None, None, None),
            P("ta", "gz", "xy", None, None, None),
            P("ta", "gz", "xy", None),
            P("xy", None),
        ),
        out_specs=(P("ta", "gz", "xy", None, None, None), P("ta", "gz", "xy", None, None, None)),
        check_vma=False,
    )
```

profile of v0, /device:TPU:1, one launch (start us, length us, event | category | flops | bytes accessed | tf_op | source)
XLA Modules:
  0.0 674.4 jit_solution(10552285033728135520)
XLA Ops:
  7.2 0.0 copy-start
  7.2 0.0 copy-start.2
  7.2 0.0 all-reduce.4.cloned.1.call-start
  7.2 4.3 collective-permute-start.1
  11.5 3.8 collective-permute-start
  15.4 0.8 constant_dynamic-update-slice_fusion.11
  16.1 0.7 slice_bitcast_fusion.11
  16.9 0.8 constant_dynamic-update-slice_fusion.1
  17.7 2.1 collective-permute-start.3
  19.7 4.0 collective-permute-start.2
  23.8 0.8 collective-permute-done.3
  24.5 0.2 collective-permute-done.2
  24.7 3.1 collective-permute-start.5
  27.8 8.6 %collective-permute-start.4 = (f32[3,3,1,2,32,128]{5,4,3,2,1,0:T(8,128)S(1)}, f32[3,3,1,2,32,128]{5,4,3,2,1,0:T(8,128)S(1)}, u32[]{:S(2)}, u32[]{:S(2)}) collective-permute-start(f32[3,3,1,2,32,128]{5,4,3,2,1,0:T(8,128)S(1)} %pad_maximum_fusion), channel_id=1, source_target_pairs={{1,0},{2,1},{3,2},{4,3},{5,4},{6,5},{7,6},{0,7},{9,8},{10,9},{11,1... | collective-permute-start | bytes 884744 | tf_op jit(solution)/shard_map/ppermute | solution.py:16
  36.4 6.2 collective-permute-done.4
  42.7 1.4 fusion.6
  44.1 0.1 fusion.13
  44.2 100.0 %all-reduce.1 = (f32[32]{0:T(128)S(1)}, f32[32]{0:T(128)S(1)}) all-reduce(f32[32]{0:T(128)S(1)} %get-tuple-element.14, f32[32]{0:T(128)S(1)} %fusion.13), channel_id=1, replica_groups=mesh['ta'=8,'gz'=8,'xy'=8] {'ta','gz','xy'}, use_global_device_ids=true, to_apply=%region_1.2 | all-reduce | flops 64 | bytes 512 | tf_op jit(solution)/shard_map/psum | solution.py:52
  144.2 0.1 constant_dynamic-update-slice_fusion.20
  144.3 2.4 collective-permute-start.7
  146.7 4.1 collective-permute-start.6
  150.8 1.2 collective-permute-done.6
  152.0 2.3 collective-permute-start.9
  154.3 1.6 collective-permute-done.9
  155.9 2.7 collective-permute-done.8
  158.6 0.0 copy-start.4
  158.6 0.0 copy-start.5
  158.6 2.7 collective-permute-start.11
  161.4 3.8 collective-permute-start.10
  165.2 5.9 collective-permute-done.10
  171.1 1.4 fusion.14
  172.5 98.7 %psum.44 = f32[32]{0:T(128)S(1)} all-reduce(f32[32]{0:T(128)S(1)} %get-tuple-element.16), channel_id=1, replica_groups=mesh['ta'=8,'gz'=8,'xy'=8] {'ta','gz','xy'}, use_global_device_ids=true, to_apply=%region_5.6 | all-reduce | flops 32 | bytes 256 | tf_op jit(solution)/shard_map/psum | solution.py:59
  271.2 0.2 multiply_reduce_fusion
  271.4 0.1 fusion.11
  271.5 94.5 %all-reduce = (f32[32]{0:T(128)S(1)}, f32[32]{0:T(128)S(1)}) all-reduce(f32[32]{0:T(128)S(1)} %fusion.11, f32[32]{0:T(128)S(1)} %get-tuple-element.6), channel_id=1, replica_groups=mesh['ta'=8,'gz'=8,'xy'=8] {'ta','gz','xy'}, use_global_device_ids=true, to_apply=%region_7.8 | all-reduce | flops 64 | bytes 512 | tf_op jit(solution)/shard_map/psum | solution.py:63
  366.0 0.1 bitcast_subtract_fusion
  366.1 0.2 fusion.8
  366.3 1.4 convolution_bitcast_fusion
  367.7 1.4 copy.19
  369.1 1.2 reshape.34
  370.3 0.0 all-reduce.4.cloned.1.call-update
  370.4 267.4 %all-reduce.4.cloned.1.call-done = f32[2048,32]{0,1:T(8,128)} async-done(((f32[2048,32]{0,1:T(8,128)}), f32[2048,32]{0,1:T(8,128)}) %all-reduce.4.cloned.1.call-update) | async-done | bytes 262160 | tf_op jit(solution)/shard_map/psum | solution.py:83
  637.7 2.9 convolution_bitcast_fusion.2
  640.6 21.4 %all_gather.3 = f32[2048,32]{0,1:T(8,128)} all-gather(f32[256,32]{0,1:T(8,128)S(1)} %convolution_bitcast_fusion.2), channel_id=1, replica_groups=mesh['ta'=8,'gz'=8,'xy'=8] {'xy'}, dimensions={0}, use_global_device_ids=true | all-gather | bytes 294912 | tf_op jit(solution)/shard_map/all_gather | solution.py:90
  662.0 1.3 reshape.35
  663.3 1.2 copy.24
  664.5 2.2 fusion.17
  666.7 0.9 fusion.5
  (39 shorter events, 0.2 us)
Async XLA Ops:
  7.2 630.6 %copy-start = (f32[256,2048]{1,0:T(8,128)S(1)}, f32[256,2048]{1,0:T(8,128)}, u32[]{:S(2)}) copy-start(f32[256,2048]{1,0:T(8,128)} %param.9) | copy-start | bytes 6291460
  7.2 35.5 %copy-start.2 = (f32[1,1,1,2,32,128]{5,4,3,2,1,0:T(8,128)S(1)}, f32[1,1,1,2,32,128]{5,4,3,2,1,0:T(8,128)}, u32[]{:S(2)}) copy-start(f32[1,1,1,2,32,128]{5,4,3,2,1,0:T(8,128)} %param.5) | copy-start | bytes 98308
  7.2 35.5 %copy-start.1 = (f32[1,1,1,2,9,128,128]{6,5,4,3,2,1,0:T(8,128)S(1)}, f32[1,1,1,2,9,128,128]{6,5,4,3,2,1,0:T(8,128)}, u32[]{:S(2)}) copy-start(f32[1,1,1,2,9,128,128]{6,5,4,3,2,1,0:T(8,128)} %param.6) | copy-start | bytes 3538948
  7.2 630.5 %all-reduce.4.cloned.1.call-start = ((), (), s32[]{:S(2)}) async-start(), calls=%async_computation | async-start | bytes 524288 | tf_op jit(solution)/shard_map/psum | solution.py:83
  7.2 9.6 %collective-permute-start.1 = (f32[1,1,1,2,32,128]{5,4,3,2,1,0:T(8,128)}, f32[1,1,1,2,32,128]{5,4,3,2,1,0:T(8,128)S(1)}, u32[]{:S(2)}, u32[]{:S(2)}) collective-permute-start(f32[1,1,1,2,32,128]{5,4,3,2,1,0:T(8,128)} %param.5), channel_id=1, source_target_pairs={{0,64},{64,128},{128,192},{192,256},{256,320},{320,384},{384,448},... | collective-permute-start | bytes 98312 | tf_op jit(solution)/shard_map/ppermute | solution.py:14
  11.5 6.1 collective-permute-start
  17.7 6.9 %collective-permute-start.3 = (f32[3,1,1,2,32,128]{5,4,3,2,1,0:T(8,128)S(1)}, f32[3,1,1,2,32,128]{5,4,3,2,1,0:T(8,128)S(1)}, u32[]{:S(2)}, u32[]{:S(2)}) collective-permute-start(f32[3,1,1,2,32,128]{5,4,3,2,1,0:T(8,128)S(1)} %constant_dynamic-update-slice_fusion), channel_id=1, source_target_pairs={{0,8},{8,16},{16,24},{24,32},{32,40},{40,48},{48,56},{56,0},{1,9},... | collective-permute-start | bytes 294920 | tf_op jit(solution)/shard_map/ppermute | solution.py:14
  19.7 5.0 collective-permute-start.2
  24.7 17.9 %collective-permute-start.5 = (f32[3,3,1,2,32,128]{5,4,3,2,1,0:T(8,128)S(1)}, f32[3,3,1,2,32,128]{5,4,3,2,1,0:T(8,128)S(1)}, u32[]{:S(2)}, u32[]{:S(2)}) collective-permute-start(f32[3,3,1,2,32,128]{5,4,3,2,1,0:T(8,128)S(1)} %pad_maximum_fusion), channel_id=1, source_target_pairs={{0,1},{1,2},{2,3},{3,4},{4,5},{5,6},{6,7},{7,0},{8,9},{9,10},{10,1... | collective-permute-start | bytes 884744 | tf_op jit(solution)/shard_map/ppermute | solution.py:14
  27.8 14.8 %collective-permute-start.4 = (f32[3,3,1,2,32,128]{5,4,3,2,1,0:T(8,128)S(1)}, f32[3,3,1,2,32,128]{5,4,3,2,1,0:T(8,128)S(1)}, u32[]{:S(2)}, u32[]{:S(2)}) collective-permute-start(f32[3,3,1,2,32,128]{5,4,3,2,1,0:T(8,128)S(1)} %pad_maximum_fusion), channel_id=1, source_target_pairs={{1,0},{2,1},{3,2},{4,3},{5,4},{6,5},{7,6},{0,7},{9,8},{10,9},{11,1... | collective-permute-start | bytes 884744 | tf_op jit(solution)/shard_map/ppermute | solution.py:16
  144.3 6.5 collective-permute-start.7
  146.7 5.3 collective-permute-start.6
  152.0 3.9 collective-permute-start.9
  154.3 4.3 collective-permute-start.8
  158.6 207.5 %copy-start.4 = (f32[1,1,1,2,32,128]{5,4,3,2,1,0:T(8,128)S(1)}, f32[1,1,1,2,32,128]{5,4,3,2,1,0:T(8,128)}, u32[]{:S(2)}) copy-start(f32[1,1,1,2,32,128]{5,4,3,2,1,0:T(8,128)} %param.7) | copy-start | bytes 98308
  158.6 207.7 %copy-start.5 = (s32[1,1,1,2]{3,2,1,0:T(1,128)S(1)}, s32[1,1,1,2]{3,2,1,0:T(1,128)}, u32[]{:S(2)}) copy-start(s32[1,1,1,2]{3,2,1,0:T(1,128)} %param.8) | copy-start | bytes 28
  158.6 12.4 %collective-permute-start.11 = (f32[3,3,1,2,32,128]{5,4,3,2,1,0:T(8,128)S(1)}, f32[3,3,1,2,32,128]{5,4,3,2,1,0:T(8,128)S(1)}, u32[]{:S(2)}, u32[]{:S(2)}) collective-permute-start(f32[3,3,1,2,32,128]{5,4,3,2,1,0:T(8,128)S(1)} %pad_maximum_fusion.1), channel_id=1, source_target_pairs={{0,1},{1,2},{2,3},{3,4},{4,5},{5,6},{6,7},{7,0},{8,9},{9,10},{10,1... | collective-permute-start | bytes 884744 | tf_op jit(solution)/shard_map/ppermute | solution.py:14
  161.4 9.7 %collective-permute-start.10 = (f32[3,3,1,2,32,128]{5,4,3,2,1,0:T(8,128)S(1)}, f32[3,3,1,2,32,128]{5,4,3,2,1,0:T(8,128)S(1)}, u32[]{:S(2)}, u32[]{:S(2)}) collective-permute-start(f32[3,3,1,2,32,128]{5,4,3,2,1,0:T(8,128)S(1)} %pad_maximum_fusion.1), channel_id=1, source_target_pairs={{1,0},{2,1},{3,2},{4,3},{5,4},{6,5},{7,6},{0,7},{9,8},{10,9},{11,1... | collective-permute-start | bytes 884744 | tf_op jit(solution)/shard_map/ppermute | solution.py:16
  366.1 4.2 copy-start.3
Sparse Core Ops, SparseCore 0:
  370.5 267.1 all-reduce.3
where the time goes:
time: 680 us; the launch traced here: 674 us
  blocking collectives  315 us (46%)
  waiting for transfers between devices  286 us (42%)
  starting transfers between devices  41.1 us (6%)
  between operations  14.3 us (2%)
  matrix products  10.4 us (2%)
  local copies, waits for them, and re-layouts  7.46 us (1%)
    psum x1, waiting for transfers between devices, body(): coarse_rhs = lax.psum(partial_rhs, ('ta', 'gz', 'xy'))  267 us
    psum x1, blocking collectives, body(): lax.psum((inner_sum(image_first, right_side), inner_sum(image_first, imag...  100 us
    psum x1, blocking collectives, body(): lax.psum(inner_sum(image_first, image_raw), ('ta', 'gz', 'xy'))  98.7 us
    psum x1, blocking collectives, body(): lax.psum((inner_sum(image_second, resid_mid), inner_sum(image_second, ima...  94.5 us
    ppermute x6, starting transfers between devices, extended(): lax.ppermute(head, axis, [((i + 1) % count, i) for i in range(count)])  24.3 us
    all_gather x1, blocking collectives, body(): correction = lax.all_gather(rows_part, 'xy', axis=0, tiled=True)  21.4 us
    ppermute x6, starting transfers between devices, extended(): lax.ppermute(tail, axis, [(i, (i + 1) % count) for i in range(count)])  16.8 us
    ppermute x6, waiting for transfers between devices, extended(): lax.ppermute(head, axis, [((i + 1) % count, i) for i in range(count)])  16.1 us
  transfers between devices with their start and end apart: 13, of which 8 were waited for; matrix products, arithmetic and copies ran while one was open for 0% of the time, Pallas kernels for 0%

commit v1 on v0

v1 whole, which is shorter than its diff:
```python
import jax
import jax.numpy as jnp
from jax import lax
from jax.experimental import pallas as pl
from jax.experimental.pallas import tpu as pltpu
from jax.sharding import PartitionSpec as P

AXES = ("ta", "gz", "xy")
HIGHEST = lax.Precision.HIGHEST
F32 = jnp.float32
NT = (((1,), (1,)), ((), ()))
NN = (((1,), (0,)), ((), ()))


def dot(left, right, dims):
    return lax.dot_general(left, right, dims, precision=HIGHEST, preferred_element_type=F32)


def halo(field):
    sides = []
    for axis in AXES:
        count = lax.axis_size(axis)
        for step in (1, -1):
            sides.append(
                lax.ppermute(field, axis, [((i + step) % count, i) for i in range(count)])
            )
    return sides


def operator(field, sides, stencil, site):
    total = dot(field[site], stencil[site, 0], NT)
    for place, side in enumerate(sides):
        total = total + dot(side[site], stencil[site, 1 + place], NT)
    both = stencil[site, 7] + stencil[site, 8]
    return total + dot(field[1 - site], both, NT)


def first_kernel(field, s0, s1, s2, s3, s4, s5, stencil, image, differ):
    for site in range(2):
        value = operator(field, (s0, s1, s2, s3, s4, s5), stencil, site)
        image[site] = value
        differ[site] = field[site] - value


def second_kernel(
    label, differ, s0, s1, s2, s3, s4, s5, stencil, image, vectors, image_two, send
):
    rhs = differ.shape[1]
    lane = lax.broadcasted_iota(jnp.int32, (rhs, 128), 1)
    zero = jnp.zeros((32, 128), F32)
    packed = jnp.zeros((rhs, 128), F32)
    sums = [jnp.zeros((rhs, 1), F32) for _ in range(5)]
    for site in range(2):
        u, w = differ[site], image[site]
        q = operator(differ, (s0, s1, s2, s3, s4, s5), stencil, site)
        image_two[site] = q
        rows = vectors[site]
        packed = packed + dot(u, jnp.concatenate([rows, zero, zero, zero], axis=0), NT)
        packed = packed + dot(w, jnp.concatenate([zero, rows, zero, zero], axis=0), NT)
        packed = packed + dot(q, jnp.concatenate([zero, zero, rows, zero], axis=0), NT)
        for place, (one, other) in enumerate(((w, w), (w, u), (w, q), (q, u), (q, q))):
            sums[place] = sums[place] + jnp.sum(one * other, axis=1, keepdims=True)
    for place in range(5):
        packed = jnp.where(lane == 96 + place, sums[place], packed)
    packed = jnp.where(lane == 101, label[0].astype(F32), packed)
    for right in range(rhs):
        send[right] = jnp.broadcast_to(packed[right : right + 1, :], (16, 128))


def coarse_kernel(first_label, recv, inverse, send):
    lane = lax.broadcasted_iota(jnp.int32, (1, 128), 1)
    blocks = recv[...].reshape(4, 2, 4, 2, 8, 128)
    part = blocks[:, 0] + blocks[:, 1]
    part = part[:, :, 0] + part[:, :, 1]
    part = part.reshape(128, 128)
    total = jnp.sum(part, axis=0, keepdims=True)

    def pick(row, place):
        return jnp.sum(jnp.where(lane == place, row, 0.0), axis=1, keepdims=True)

    ww, wu, wq, qu, qq = [pick(total, 96 + place) for place in range(5)]
    first = wu / ww
    gamma = wq / ww
    sigma = (qu - gamma * wu) / (qq - gamma * wq)
    kappa = sigma * gamma - first
    labels = pick(part, 101) * 0.25
    mixed = part + kappa * pltpu.roll(part, 96, 1) - sigma * pltpu.roll(part, 64, 1)
    mixed = jnp.where(lane < 32, mixed, 0.0)
    mixed = mixed + pltpu.roll(mixed, 32, 1)
    mixed = mixed + pltpu.roll(mixed, 64, 1)
    group = (lane // 32).astype(F32)
    rows = []
    for place in range(16):
        chosen = labels == group + 4.0 * place
        rows.append(jnp.sum(jnp.where(chosen, mixed, 0.0), axis=0, keepdims=True))
    pieces = []
    for start in range(0, 256, 64):
        piece = inverse[start : start + 64, 0:128] * rows[0]
        for place in range(1, 16):
            piece = piece + inverse[start : start + 64, 128 * place : 128 * place + 128] * rows[place]
        pieces.append(piece)
    solved = jnp.concatenate(pieces, axis=0)
    halves = []
    for half in range(2):
        halves.append(
            jnp.sum(jnp.transpose(solved[128 * half : 128 * half + 128]), axis=0, keepdims=True)
        )
    scalars = jnp.where(lane == 32, sigma, jnp.where(lane == 33, kappa, 0.0))
    base = first_label[0].astype(F32)
    out = jnp.zeros((128, 128), F32)
    for place in range(8):
        row = halves[place // 4]
        if place % 4:
            row = pltpu.roll(row, 128 - 32 * (place % 4), 1)
        row = jnp.where(lane < 32, row, scalars)
        out = jnp.where(labels == base + float(place), row, out)
    out = out.reshape(4, 4, 8, 128)
    for t in range(8):
        for z in range(8):
            send[t, z] = out[t // 2, z // 2]


def last_kernel(recv, field, differ, image, image_two, vectors, solved, residual):
    got = jnp.concatenate(
        [
            jnp.sum(recv[t, z], axis=0, keepdims=True)
            for t in range(8)
            for z in range(0, 8, 2)
        ],
        axis=0,
    )
    correction = got[:, 0:32]
    sigma, kappa = got[:, 32:33], got[:, 33:34]
    for site in range(2):
        b, u, w, q = field[site], differ[site], image[site], image_two[site]
        residual[site] = u + kappa * w - sigma * q
        solved[site] = (1.0 - kappa) * b + sigma * u + dot(correction, vectors[site], NN)


def call(kernel, scalars, arrays, outs, name):
    shapes = [jax.ShapeDtypeStruct(shape, F32) for shape in outs]
    return pl.pallas_call(
        kernel,
        out_shape=shapes,
        in_specs=[pl.BlockSpec(memory_space=pltpu.SMEM)] * len(scalars)
        + [pl.BlockSpec(memory_space=pltpu.VMEM)] * len(arrays),
        out_specs=[pl.BlockSpec(memory_space=pltpu.VMEM)] * len(outs),
        compiler_params=pltpu.CompilerParams(vmem_limit_bytes=16 * 1024 * 1024),
        name=name,
    )(*scalars, *arrays)


def body(right_side, stencil, restrict, aggregate, coarsest_inverse):
    field = right_side[0, 0, 0]
    blocks = stencil[0, 0, 0]
    vectors = restrict[0, 0, 0]
    local = field.shape
    image, differ = call(
        first_kernel, (), (field, *halo(field), blocks), (local, local), "first_image"
    )
    image_two, send = call(
        second_kernel,
        (aggregate.reshape(2),),
        (differ, *halo(differ), blocks, image, vectors),
        (local, (32, 16, 128)),
        "second_image",
    )
    recv = lax.all_to_all(send.reshape(512, 128), AXES, 0, 0, tiled=True)
    first_label = (lax.axis_index("xy") * 8).astype(jnp.int32).reshape(1)
    (back,) = call(
        coarse_kernel,
        (first_label,),
        (recv.reshape(8, 8, 8, 128), coarsest_inverse),
        ((8, 8, 8, 128),),
        "coarse_solve",
    )
    home = lax.all_to_all(back.reshape(512, 128), AXES, 0, 0, tiled=True)
    solved, residual = call(
        last_kernel,
        (),
        (home.reshape(8, 8, 8, 128), field, differ, image, image_two, vectors),
        (local, local),
        "last_update",
    )
    return solved[None, None, None], residual[None, None, None]


def solution(mesh):
    return jax.shard_map(
        body,
        mesh=mesh,
        in_specs=(
            P("ta", "gz", "xy", None, None, None),
            P("ta", "gz", "xy", None, None, None, None),
            P("ta", "gz", "xy", None, None, None),
            P("ta", "gz", "xy", None),
            P("xy", None),
        ),
        out_specs=(P("ta", "gz", "xy", None, None, None), P("ta", "gz", "xy", None, None, None)),
        check_vma=False,
    )
```

time: 680 us -> 112 us (0.16)
  blocking collectives: 315 us -> 26 us
  waiting for transfers between devices: 286 us -> 23.3 us
  between operations: 14.3 us -> 0.77 us
  matrix products: 10.4 us -> 0 us
  starting transfers between devices: 41.1 us -> 49.6 us
  Pallas kernels: 0 us -> 8.24 us
    psum x3 -> x0, blocking collectives: 293 us -> none  [the longest x1 100 us: body(): lax.psum((inner_sum(image_first, right_side), inner_sum(image_first, imag...]
    psum x1 -> x0, waiting for transfers between devices: 267 us -> none  [body(): coarse_rhs = lax.psum(partial_rhs, ('ta', 'gz', 'xy'))]
    all_to_all x0 -> x1, blocking collectives: none -> 26 us  [body(): home = lax.all_to_all(back.reshape(512, 128), AXES, 0, 0, tiled=True)]
    all_gather x1 -> x0, blocking collectives: 21.4 us -> none  [body(): correction = lax.all_gather(rows_part, 'xy', axis=0, tiled=True)]
    all_to_all x0 -> x1, waiting for transfers between devices: none -> 17.6 us  [body(): recv = lax.all_to_all(send.reshape(512, 128), AXES, 0, 0, tiled=True)]
    ppermute x12, waiting for transfers between devices: 18.5 us -> 5.69 us  [halo(): lax.ppermute(field, axis, [((i + step) % count, i) for i in range(count)])]
    all_to_all x0 -> x1, starting transfers between devices: none -> 12 us  [body(): recv = lax.all_to_all(send.reshape(512, 128), AXES, 0, 0, tiled=True)]
    dot_general x7 -> x0, matrix products: 10.4 us -> none  [the longest x1 2.88 us: body(): jnp.dot(coarsest_inverse, coarse_rhs, precision=lax.Precision.HIGHEST, pr...]
  transfers between devices with their start and end apart: 13 -> 13, of which waited for: 8 -> 4; matrix products, arithmetic and copies ran while one was open for 0% -> 0% of each run, Pallas kernels for 0% -> 0%
where the time goes in v1:
time: 112 us; the launch traced here: 111 us
  starting transfers between devices  49.6 us (44%)
  blocking collectives  26 us (23%)
  waiting for transfers between devices  23.3 us (21%)
  Pallas kernels  8.24 us (7%)
  local copies, waits for them, and re-layouts  3.45 us (3%)
    ppermute x12, starting transfers between devices, halo(): lax.ppermute(field, axis, [((i + step) % count, i) for i in range(count)])  37.6 us
    all_to_all x1, blocking collectives, body(): home = lax.all_to_all(back.reshape(512, 128), AXES, 0, 0, tiled=True)  26 us
    all_to_all x1, waiting for transfers between devices, body(): recv = lax.all_to_all(send.reshape(512, 128), AXES, 0, 0, tiled=True)  17.6 us
    all_to_all x1, starting transfers between devices, body(): recv = lax.all_to_all(send.reshape(512, 128), AXES, 0, 0, tiled=True)  12 us
    pallas_call x4, Pallas kernels, call(): pl.pallas_call(kernel, out_shape=shapes, in_specs=[pl.BlockSpec(memory_sp...  8.24 us
    ppermute x12, waiting for transfers between devices, halo(): lax.ppermute(field, axis, [((i + step) % count, i) for i in range(count)])  5.69 us
    unnamed x16, local copies, waits for them, and re-layouts  3.45 us
  transfers between devices with their start and end apart: 13, of which 4 were waited for; matrix products, arithmetic and copies ran while one was open for 0% of the time, Pallas kernels for 0%

profile of v1, /device:TPU:1, one launch (start us, length us, event | category | flops | bytes accessed | tf_op | source)
XLA Modules:
  0.0 111.3 jit_solution(13854748478021457063)
XLA Ops:
  0.6 5.9 %collective-permute-start = (f32[2,32,128]{2,1,0:T(8,128)}, f32[2,32,128]{2,1,0:T(8,128)S(1)}, u32[]{:S(2)}, u32[]{:S(2)}) collective-permute-start(f32[2,32,128]{2,1,0:T(8,128)} %bitcast.20), channel_id=1, source_target_pairs={{64,0},{128,64},{192,128},{256,192},{320,256},{384,320},{448,384},... | collective-permute-start | bytes 98312 | tf_op jit(solution)/shard_map/ppermute | solution.py:25
  6.6 1.9 %collective-permute-start.1 = (f32[2,32,128]{2,1,0:T(8,128)}, f32[2,32,128]{2,1,0:T(8,128)S(1)}, u32[]{:S(2)}, u32[]{:S(2)}) collective-permute-start(f32[2,32,128]{2,1,0:T(8,128)} %bitcast.21), channel_id=1, source_target_pairs={{448,0},{0,64},{64,128},{128,192},{192,256},{256,320},{320,384},{3... | collective-permute-start | bytes 98312 | tf_op jit(solution)/shard_map/ppermute | solution.py:25
  8.5 4.9 %collective-permute-start.2 = (f32[2,32,128]{2,1,0:T(8,128)}, f32[2,32,128]{2,1,0:T(8,128)S(1)}, u32[]{:S(2)}, u32[]{:S(2)}) collective-permute-start(f32[2,32,128]{2,1,0:T(8,128)} %bitcast.22), channel_id=1, source_target_pairs={{8,0},{16,8},{24,16},{32,24},{40,32},{48,40},{56,48},{0,56},{9,1},... | collective-permute-start | bytes 98312 | tf_op jit(solution)/shard_map/ppermute | solution.py:25
  13.3 0.0 collective-permute-start.3
  13.3 7.9 %collective-permute-start.4 = (f32[2,32,128]{2,1,0:T(8,128)}, f32[2,32,128]{2,1,0:T(8,128)S(1)}, u32[]{:S(2)}, u32[]{:S(2)}) collective-permute-start(f32[2,32,128]{2,1,0:T(8,128)} %bitcast.24), channel_id=1, source_target_pairs={{1,0},{2,1},{3,2},{4,3},{5,4},{6,5},{7,6},{0,7},{9,8},{10,9},{11,1... | collective-permute-start | bytes 98312 | tf_op jit(solution)/shard_map/ppermute | solution.py:25
  21.2 0.0 collective-permute-done.s0
  21.3 1.9 %collective-permute-start.5 = (f32[2,32,128]{2,1,0:T(8,128)}, f32[2,32,128]{2,1,0:T(8,128)S(1)}, u32[]{:S(2)}, u32[]{:S(2)}) collective-permute-start(f32[2,32,128]{2,1,0:T(8,128)} %bitcast.25), channel_id=1, source_target_pairs={{7,0},{0,1},{1,2},{2,3},{3,4},{4,5},{5,6},{6,7},{15,8},{8,9},{9,10... | collective-permute-start | bytes 98312 | tf_op jit(solution)/shard_map/ppermute | solution.py:25
  23.2 0.0 collective-permute-done.1.s1
  23.2 0.0 collective-permute-done.2.s2
  23.2 0.0 collective-permute-done.3.s3
  23.2 0.0 collective-permute-done.4.s4
  23.2 4.1 %collective-permute-done.5.s5 = f32[2,32,128]{2,1,0:T(8,128)S(1)} collective-permute-done((f32[2,32,128]{2,1,0:T(8,128)}, f32[2,32,128]{2,1,0:T(8,128)S(1)}, u32[]{:S(2)}, u32[]{:S(2)}) %collective-permute-start.5) | collective-permute-done | bytes 32800 | tf_op jit(solution)/shard_map/ppermute | solution.py:25
  27.3 0.0 copy-start
  27.3 1.3 %copy-done = f32[1,1,1,2,9,128,128]{6,5,4,3,2,1,0:T(8,128)S(1)} copy-done((f32[1,1,1,2,9,128,128]{6,5,4,3,2,1,0:T(8,128)S(1)}, f32[1,1,1,2,9,128,128]{6,5,4,3,2,1,0:T(8,128)}, u32[]{:S(2)}) %copy-start) | copy-done | bytes 1179672
  28.6 0.0 copy-start.3
  28.6 0.8 copy-done.3
  29.4 0.0 copy-start.1
  29.4 0.0 copy-start.2
  29.4 1.7 %first_image.1 = (f32[2,32,128]{2,1,0:T(8,128)S(1)}, f32[2,32,128]{2,1,0:T(8,128)S(1)}) custom-call(f32[2,32,128]{2,1,0:T(8,128)S(1)} %bitcast.26, f32[2,32,128]{2,1,0:T(8,128)S(1)} %collective-permute-done.s0, f32[2,32,128]{2,1,0:T(8,128)S(1)} %collective-permute-done.1.s1, f32[2,32,128]{2,1,0:T(8,128)S(1)} %collective-permute-done.2.s2, ...), custom_call_target="tpu_custom_call" | custom-call | tf_op jit(solution)/shard_map/first_image/pallas_call | solution.py:142
  31.1 1.9 %collective-permute-start.10 = (f32[2,32,128]{2,1,0:T(8,128)S(1)}, f32[2,32,128]{2,1,0:T(8,128)S(1)}, u32[]{:S(2)}, u32[]{:S(2)}) collective-permute-start(f32[2,32,128]{2,1,0:T(8,128)S(1)} %get-tuple-element.8.differ), channel_id=1, source_target_pairs={{1,0},{2,1},{3,2},{4,3},{5,4},{6,5},{7,6},{0,7},{9,8},{10,9},{11,1... | collective-permute-start | bytes 98312 | tf_op jit(solution)/shard_map/ppermute | solution.py:25
  33.0 3.4 %collective-permute-start.11 = (f32[2,32,128]{2,1,0:T(8,128)S(1)}, f32[2,32,128]{2,1,0:T(8,128)S(1)}, u32[]{:S(2)}, u32[]{:S(2)}) collective-permute-start(f32[2,32,128]{2,1,0:T(8,128)S(1)} %get-tuple-element.8.differ), channel_id=1, source_target_pairs={{7,0},{0,1},{1,2},{2,3},{3,4},{4,5},{5,6},{6,7},{15,8},{8,9},{9,10... | collective-permute-start | bytes 98312 | tf_op jit(solution)/shard_map/ppermute | solution.py:25
  36.4 4.9 %collective-permute-start.6 = (f32[2,32,128]{2,1,0:T(8,128)S(1)}, f32[2,32,128]{2,1,0:T(8,128)S(1)}, u32[]{:S(2)}, u32[]{:S(2)}) collective-permute-start(f32[2,32,128]{2,1,0:T(8,128)S(1)} %get-tuple-element.8.differ), channel_id=1, source_target_pairs={{64,0},{128,64},{192,128},{256,192},{320,256},{384,320},{448,384},... | collective-permute-start | bytes 98312 | tf_op jit(solution)/shard_map/ppermute | solution.py:25
  41.3 1.9 %collective-permute-start.7 = (f32[2,32,128]{2,1,0:T(8,128)S(1)}, f32[2,32,128]{2,1,0:T(8,128)S(1)}, u32[]{:S(2)}, u32[]{:S(2)}) collective-permute-start(f32[2,32,128]{2,1,0:T(8,128)S(1)} %get-tuple-element.8.differ), channel_id=1, source_target_pairs={{448,0},{0,64},{64,128},{128,192},{192,256},{256,320},{320,384},{3... | collective-permute-start | bytes 98312 | tf_op jit(solution)/shard_map/ppermute | solution.py:25
  43.2 2.8 %collective-permute-start.8 = (f32[2,32,128]{2,1,0:T(8,128)S(1)}, f32[2,32,128]{2,1,0:T(8,128)S(1)}, u32[]{:S(2)}, u32[]{:S(2)}) collective-permute-start(f32[2,32,128]{2,1,0:T(8,128)S(1)} %get-tuple-element.8.differ), channel_id=1, source_target_pairs={{8,0},{16,8},{24,16},{32,24},{40,32},{48,40},{56,48},{0,56},{9,1},... | collective-permute-start | bytes 98312 | tf_op jit(solution)/shard_map/ppermute | solution.py:25
  46.0 0.0 collective-permute-done.10.s4
  46.0 0.2 collective-permute-start.9
  46.2 0.0 collective-permute-done.11.s5
  46.2 0.0 collective-permute-done.6.s0
  46.2 0.9 collective-permute-done.7.s1
  47.1 0.6 collective-permute-done.8.s2
  47.8 0.0 collective-permute-done.9.s3
  47.8 0.0 copy-done.1
  47.8 0.0 copy-start.5
  47.8 0.8 copy-done.5
  48.5 0.0 copy-start.7
  48.5 0.7 copy-done.7
  49.2 4.9 %second_image.1 = (f32[2,32,128]{2,1,0:T(8,128)S(1)}, f32[32,16,128]{2,1,0:T(8,128)}) custom-call(s32[2]{0:T(128)S(1)} %bitcast.30, f32[2,32,128]{2,1,0:T(8,128)S(1)} %get-tuple-element.8.differ, f32[2,32,128]{2,1,0:T(8,128)S(1)} %collective-permute-done.6.s0, f32[2,32,128]{2,1,0:T(8,128)S(1)} %collective-permute-done.7.s1, ...), custom_call_target="tpu_custom_call" | custom-call | tf_op jit(solution)/shard_map/second_image/pallas_call | solution.py:142
  54.1 0.0 copy-start.4
  54.1 0.0 copy-start.6
  54.1 12.0 %all-to-all-start = ((f32[512,1,128]{2,1,0:T(1,128)}), f32[512,1,128]{2,1,0:T(1,128)S(1)}, u32[]{:S(2)}, u32[]{:S(2)}) async-start(f32[512,1,128]{2,1,0:T(1,128)} %bitcast.6), calls=%async_computation | async-start | bytes 524288 | tf_op jit(solution)/shard_map/all_to_all | solution.py:168
  66.1 17.6 %all-to-all-done = f32[512,1,128]{2,1,0:T(1,128)S(1)} async-done(((f32[512,1,128]{2,1,0:T(1,128)}), f32[512,1,128]{2,1,0:T(1,128)S(1)}, u32[]{:S(2)}, u32[]{:S(2)}) %all-to-all-start) | async-done | bytes 262176 | tf_op jit(solution)/shard_map/all_to_all | solution.py:168
  83.6 0.0 copy-done.2
  83.6 0.8 coarse_solve.1
  84.5 26.0 %all_to_all.18 = f32[512,1,128]{2,1,0:T(1,128)S(1)} all-to-all(f32[512,1,128]{2,1,0:T(1,128)S(1)} %bitcast.19), channel_id=1, replica_groups=mesh['ta'=8,'gz'=8,'xy'=8] {'ta','gz','xy'}, dimensions={0} | all-to-all | bytes 524288 | tf_op jit(solution)/shard_map/all_to_all | solution.py:177
  110.5 0.0 copy-done.4
  110.5 0.0 copy-done.6
  110.5 0.8 last_update.1
Async XLA Ops:
  0.6 20.6 %collective-permute-start = (f32[2,32,128]{2,1,0:T(8,128)}, f32[2,32,128]{2,1,0:T(8,128)S(1)}, u32[]{:S(2)}, u32[]{:S(2)}) collective-permute-start(f32[2,32,128]{2,1,0:T(8,128)} %bitcast.20), channel_id=1, source_target_pairs={{64,0},{128,64},{192,128},{256,192},{320,256},{384,320},{448,384},... | collective-permute-start | bytes 98312 | tf_op jit(solution)/shard_map/ppermute | solution.py:25
  6.6 16.6 %collective-permute-start.1 = (f32[2,32,128]{2,1,0:T(8,128)}, f32[2,32,128]{2,1,0:T(8,128)S(1)}, u32[]{:S(2)}, u32[]{:S(2)}) collective-permute-start(f32[2,32,128]{2,1,0:T(8,128)} %bitcast.21), channel_id=1, source_target_pairs={{448,0},{0,64},{64,128},{128,192},{192,256},{256,320},{320,384},{3... | collective-permute-start | bytes 98312 | tf_op jit(solution)/shard_map/ppermute | solution.py:25
  8.5 14.7 %collective-permute-start.2 = (f32[2,32,128]{2,1,0:T(8,128)}, f32[2,32,128]{2,1,0:T(8,128)S(1)}, u32[]{:S(2)}, u32[]{:S(2)}) collective-permute-start(f32[2,32,128]{2,1,0:T(8,128)} %bitcast.22), channel_id=1, source_target_pairs={{8,0},{16,8},{24,16},{32,24},{40,32},{48,40},{56,48},{0,56},{9,1},... | collective-permute-start | bytes 98312 | tf_op jit(solution)/shard_map/ppermute | solution.py:25
  13.3 9.9 %collective-permute-start.3 = (f32[2,32,128]{2,1,0:T(8,128)}, f32[2,32,128]{2,1,0:T(8,128)S(1)}, u32[]{:S(2)}, u32[]{:S(2)}) collective-permute-start(f32[2,32,128]{2,1,0:T(8,128)} %bitcast.23), channel_id=1, source_target_pairs={{56,0},{0,8},{8,16},{16,24},{24,32},{32,40},{40,48},{48,56},{57,1}... | collective-permute-start | bytes 98312 | tf_op jit(solution)/shard_map/ppermute | solution.py:25
  13.3 9.9 %collective-permute-start.4 = (f32[2,32,128]{2,1,0:T(8,128)}, f32[2,32,128]{2,1,0:T(8,128)S(1)}, u32[]{:S(2)}, u32[]{:S(2)}) collective-permute-start(f32[2,32,128]{2,1,0:T(8,128)} %bitcast.24), channel_id=1, source_target_pairs={{1,0},{2,1},{3,2},{4,3},{5,4},{6,5},{7,6},{0,7},{9,8},{10,9},{11,1... | collective-permute-start | bytes 98312 | tf_op jit(solution)/shard_map/ppermute | solution.py:25
  21.3 6.1 %collective-permute-start.5 = (f32[2,32,128]{2,1,0:T(8,128)}, f32[2,32,128]{2,1,0:T(8,128)S(1)}, u32[]{:S(2)}, u32[]{:S(2)}) collective-permute-start(f32[2,32,128]{2,1,0:T(8,128)} %bitcast.25), channel_id=1, source_target_pairs={{7,0},{0,1},{1,2},{2,3},{3,4},{4,5},{5,6},{6,7},{15,8},{8,9},{9,10... | collective-permute-start | bytes 98312 | tf_op jit(solution)/shard_map/ppermute | solution.py:25
  27.3 1.3 %copy-start = (f32[1,1,1,2,9,128,128]{6,5,4,3,2,1,0:T(8,128)S(1)}, f32[1,1,1,2,9,128,128]{6,5,4,3,2,1,0:T(8,128)}, u32[]{:S(2)}) copy-start(f32[1,1,1,2,9,128,128]{6,5,4,3,2,1,0:T(8,128)} %param.6) | copy-start | bytes 3538948
  28.6 0.8 copy-start.3
  29.4 18.4 %copy-start.1 = (f32[1,1,1,2,9,128,128]{6,5,4,3,2,1,0:T(8,128)S(1)}, f32[1,1,1,2,9,128,128]{6,5,4,3,2,1,0:T(8,128)}, u32[]{:S(2)}) copy-start(f32[1,1,1,2,9,128,128]{6,5,4,3,2,1,0:T(8,128)} %param.6) | copy-start | bytes 3538948
  29.4 54.3 %copy-start.2 = (f32[256,2048]{1,0:T(8,128)S(1)}, f32[256,2048]{1,0:T(8,128)}, u32[]{:S(2)}) copy-start(f32[256,2048]{1,0:T(8,128)} %inverse.1) | copy-start | bytes 6291460
  31.1 14.9 %collective-permute-start.10 = (f32[2,32,128]{2,1,0:T(8,128)S(1)}, f32[2,32,128]{2,1,0:T(8,128)S(1)}, u32[]{:S(2)}, u32[]{:S(2)}) collective-permute-start(f32[2,32,128]{2,1,0:T(8,128)S(1)} %get-tuple-element.8.differ), channel_id=1, source_target_pairs={{1,0},{2,1},{3,2},{4,3},{5,4},{6,5},{7,6},{0,7},{9,8},{10,9},{11,1... | collective-permute-start | bytes 98312 | tf_op jit(solution)/shard_map/ppermute | solution.py:25
  33.0 13.2 %collective-permute-start.11 = (f32[2,32,128]{2,1,0:T(8,128)S(1)}, f32[2,32,128]{2,1,0:T(8,128)S(1)}, u32[]{:S(2)}, u32[]{:S(2)}) collective-permute-start(f32[2,32,128]{2,1,0:T(8,128)S(1)} %get-tuple-element.8.differ), channel_id=1, source_target_pairs={{7,0},{0,1},{1,2},{2,3},{3,4},{4,5},{5,6},{6,7},{15,8},{8,9},{9,10... | collective-permute-start | bytes 98312 | tf_op jit(solution)/shard_map/ppermute | solution.py:25
  36.4 9.8 %collective-permute-start.6 = (f32[2,32,128]{2,1,0:T(8,128)S(1)}, f32[2,32,128]{2,1,0:T(8,128)S(1)}, u32[]{:S(2)}, u32[]{:S(2)}) collective-permute-start(f32[2,32,128]{2,1,0:T(8,128)S(1)} %get-tuple-element.8.differ), channel_id=1, source_target_pairs={{64,0},{128,64},{192,128},{256,192},{320,256},{384,320},{448,384},... | collective-permute-start | bytes 98312 | tf_op jit(solution)/shard_map/ppermute | solution.py:25
  41.3 5.9 %collective-permute-start.7 = (f32[2,32,128]{2,1,0:T(8,128)S(1)}, f32[2,32,128]{2,1,0:T(8,128)S(1)}, u32[]{:S(2)}, u32[]{:S(2)}) collective-permute-start(f32[2,32,128]{2,1,0:T(8,128)S(1)} %get-tuple-element.8.differ), channel_id=1, source_target_pairs={{448,0},{0,64},{64,128},{128,192},{192,256},{256,320},{320,384},{3... | collective-permute-start | bytes 98312 | tf_op jit(solution)/shard_map/ppermute | solution.py:25
  43.2 4.6 %collective-permute-start.8 = (f32[2,32,128]{2,1,0:T(8,128)S(1)}, f32[2,32,128]{2,1,0:T(8,128)S(1)}, u32[]{:S(2)}, u32[]{:S(2)}) collective-permute-start(f32[2,32,128]{2,1,0:T(8,128)S(1)} %get-tuple-element.8.differ), channel_id=1, source_target_pairs={{8,0},{16,8},{24,16},{32,24},{40,32},{48,40},{56,48},{0,56},{9,1},... | collective-permute-start | bytes 98312 | tf_op jit(solution)/shard_map/ppermute | solution.py:25
  46.0 1.8 %collective-permute-start.9 = (f32[2,32,128]{2,1,0:T(8,128)S(1)}, f32[2,32,128]{2,1,0:T(8,128)S(1)}, u32[]{:S(2)}, u32[]{:S(2)}) collective-permute-start(f32[2,32,128]{2,1,0:T(8,128)S(1)} %get-tuple-element.8.differ), channel_id=1, source_target_pairs={{56,0},{0,8},{8,16},{16,24},{24,32},{32,40},{40,48},{48,56},{57,1}... | collective-permute-start | bytes 98312 | tf_op jit(solution)/shard_map/ppermute | solution.py:25
  47.8 0.8 copy-start.5
  48.5 0.7 copy-start.7
  54.1 56.4 %copy-start.4 = (f32[1,1,1,2,32,128]{5,4,3,2,1,0:T(8,128)S(1)}, f32[1,1,1,2,32,128]{5,4,3,2,1,0:T(8,128)}, u32[]{:S(2)}) copy-start(f32[1,1,1,2,32,128]{5,4,3,2,1,0:T(8,128)} %param.5) | copy-start | bytes 98308
  54.1 56.4 %copy-start.6 = (f32[1,1,1,2,32,128]{5,4,3,2,1,0:T(8,128)S(1)}, f32[1,1,1,2,32,128]{5,4,3,2,1,0:T(8,128)}, u32[]{:S(2)}) copy-start(f32[1,1,1,2,32,128]{5,4,3,2,1,0:T(8,128)} %param.7) | copy-start | bytes 98308
  54.1 29.6 %all-to-all-start = ((f32[512,1,128]{2,1,0:T(1,128)}), f32[512,1,128]{2,1,0:T(1,128)S(1)}, u32[]{:S(2)}, u32[]{:S(2)}) async-start(f32[512,1,128]{2,1,0:T(1,128)} %bitcast.6), calls=%async_computation | async-start | bytes 524288 | tf_op jit(solution)/shard_map/all_to_all | solution.py:168

commit v2 on v1

v2 whole, which is shorter than its diff:
```python
import jax
import jax.numpy as jnp
from jax import lax
from jax.experimental import pallas as pl
from jax.experimental.pallas import tpu as pltpu
from jax.sharding import Mesh
from jax.sharding import PartitionSpec as P

TA, GZ, XY = ("T", "a"), ("Z", "b"), ("Y", "c")
BLOCK = ("a", "b", "c")
LATTICE = ("T", "Z", "Y")
OUTER = [(1, 2), (2, 1), (3, 4), (4, 3), (5, 6), (6, 5), (7, 0), (0, 7)]
HIGHEST = lax.Precision.HIGHEST
F32 = jnp.float32
BF16 = jnp.bfloat16
NT = (((1,), (1,)), ((), ()))
NN = (((1,), (0,)), ((), ()))


def corner():
    a, b, c = (lax.axis_index(name) for name in BLOCK)
    return (4 * (1 - a) + 2 * b + c, 4 * a + 2 * (1 - b) + c, 4 * a + 2 * b + 1 - c)


def dot(left, right, dims):
    return lax.dot_general(left, right, dims, precision=HIGHEST, preferred_element_type=F32)


def split(value):
    high = value.astype(BF16)
    return high, (value - high.astype(F32)).astype(BF16)


def prepare_kernel(stencil, weights):
    a, b, c = (lax.axis_index(name) for name in BLOCK)
    order = (1 + a, 2 - a, 3 + b, 4 - b, 5 + c, 6 - c)
    rows = lax.broadcasted_iota(jnp.int32, (128, 128), 0)
    cols = lax.broadcasted_iota(jnp.int32, (128, 128), 1)
    unit = jnp.where(rows == cols, 1.0, 0.0).astype(F32)
    for site in range(2):
        for slot in range(8):
            if slot == 0:
                block = stencil[site, 0] - unit
            elif slot == 1:
                block = stencil[site, 7] + stencil[site, 8]
            else:
                block = stencil[site, order[slot - 2]]
            high, low = split(jnp.transpose(block))
            start = 128 * (slot % 2)
            weights[site, slot // 2, start : start + 128, 0:128] = high
            weights[site, slot // 2, start : start + 128, 128:256] = low


def change(place, field, near, outer, weights, site):
    sides = [field[site], field[1 - site]]
    for axis in range(3):
        sides.append(near[place[axis], site])
        sides.append(outer[axis][site])
    total = jnp.zeros((64, 256), F32)
    for pair in range(4):
        high, low = split(jnp.concatenate(sides[2 * pair : 2 * pair + 2], axis=1))
        both = jnp.concatenate([high, low], axis=0)
        total = total + lax.dot_general(
            both, weights[site, pair], NN, preferred_element_type=F32
        )
    half = total[0:32] + total[32:64]
    return half[:, 0:128] + half[:, 128:256]


def first_kernel(field, near, o0, o1, o2, weights, image, differ, send):
    place = corner()
    for site in range(2):
        value = change(place, field, near, (o0, o1, o2), weights, site)
        image[site] = field[site] + value
        differ[site] = -value
        for other in range(8):
            send[other, site] = -value


def padded(vectors, start):
    rows = jnp.concatenate([vectors[0], vectors[1]], axis=1)
    parts = [rows]
    if start:
        parts.insert(0, jnp.zeros((start, 256), F32))
    if start < 96:
        parts.append(jnp.zeros((96 - start, 256), F32))
    return jnp.concatenate(parts, axis=0)


def inner(one, other):
    return jnp.sum(one[0] * other[0] + one[1] * other[1], axis=1, keepdims=True)


def wide(field):
    return jnp.concatenate([field[0], field[1]], axis=1)


def early_kernel(label, differ, image, vectors, packed):
    lane = lax.broadcasted_iota(jnp.int32, (32, 128), 1)
    value = dot(wide(differ), padded(vectors, 0), NT)
    value = value + dot(wide(image), padded(vectors, 32), NT)
    value = jnp.where(lane == 96, inner(image, image), value)
    value = jnp.where(lane == 97, inner(image, differ), value)
    packed[...] = jnp.where(lane == 101, label[0].astype(F32), value)


def second_kernel(
    differ, near, o0, o1, o2, weights, image, vectors, early, image_two, send
):
    lane = lax.broadcasted_iota(jnp.int32, (32, 128), 1)
    values = []
    place = corner()
    for site in range(2):
        value = differ[site] + change(place, differ, near, (o0, o1, o2), weights, site)
        image_two[site] = value
        values.append(value)
    packed = early[...] + dot(wide(values), padded(vectors, 64), NT)
    packed = jnp.where(lane == 98, inner(image, values), packed)
    packed = jnp.where(lane == 99, inner(differ, values), packed)
    packed = jnp.where(lane == 100, inner(values, values), packed)
    for group in range(4):
        for c in range(2):
            send[2 * group + c] = packed[8 * group : 8 * group + 8]


def gather_kernel(recv, send):
    total = recv[0]
    for other in range(1, 8):
        total = total + recv[other]
    for right in range(8):
        send[right] = jnp.broadcast_to(total[right : right + 1], (8, 128))


def coarse_kernel(recv, inverse, send, rows_held, arrived):
    half = lax.rem(lax.axis_index("Z"), 2)
    copies = []
    for part in range(2):
        start = pl.multiple_of(128 * half + 64 * part, 64)
        copy = pltpu.make_async_copy(
            inverse.at[pl.ds(start, 64)], rows_held.at[pl.ds(64 * part, 64)], arrived.at[part]
        )
        copy.start()
        copies.append(copy)
    lane = lax.broadcasted_iota(jnp.int32, (1, 128), 1)
    part = recv[...]
    total = jnp.sum(part, axis=0, keepdims=True)

    def pick(row, place):
        return jnp.sum(jnp.where(lane == place, row, 0.0), axis=1, keepdims=True)

    ww, wu, wq, qu, qq = [pick(total, 96 + place) for place in range(5)]
    first = wu / ww
    gamma = wq / ww
    sigma = (qu - gamma * wu) / (qq - gamma * wq)
    kappa = sigma * gamma - first
    labels = pick(part, 101) * 0.125
    mixed = part + kappa * pltpu.roll(part, 96, 1) - sigma * pltpu.roll(part, 64, 1)
    mixed = jnp.where(lane < 32, mixed, 0.0)
    mixed = mixed + pltpu.roll(mixed, 32, 1)
    mixed = mixed + pltpu.roll(mixed, 64, 1)
    group = (lane // 32).astype(F32)
    rows = []
    for place in range(16):
        chosen = labels == group + 4.0 * place
        rows.append(jnp.sum(jnp.where(chosen, mixed, 0.0), axis=0, keepdims=True))
    pieces = []
    for part in range(2):
        copies[part].wait()
        begin = 64 * part
        piece = rows_held[begin : begin + 64, 0:128] * rows[0]
        for place in range(1, 16):
            piece = piece + rows_held[begin : begin + 64, 128 * place : 128 * place + 128] * rows[place]
        pieces.append(piece)
    solved = jnp.transpose(jnp.concatenate(pieces, axis=0))
    solved = jnp.sum(solved, axis=0, keepdims=True)
    scalars = jnp.where(lane == 32, sigma, jnp.where(lane == 33, kappa, 0.0))
    base = (8 * lax.axis_index(XY) + 4 * half).astype(F32)
    out = jnp.zeros((64, 128), F32)
    for place in range(4):
        row = pltpu.roll(solved, 128 - 32 * place, 1) if place else solved
        row = jnp.where(lane < 32, row, scalars)
        out = jnp.where(labels == base + float(place), row, out)
    send[...] = out


def spread_kernel(recv, send):
    rows = []
    for right in range(8):
        rows.append(jnp.sum(recv[8 * right : 8 * right + 8], axis=0, keepdims=True))
    value = jnp.concatenate(rows, axis=0)
    for other in range(8):
        send[other] = value


def last_kernel(recv, field, differ, image, image_two, vectors, solved, residual):
    got = jnp.concatenate([recv[2 * group] + recv[2 * group + 1] for group in range(4)], axis=0)
    correction = got[:, 0:32]
    sigma, kappa = got[:, 32:33], got[:, 33:34]
    for site in range(2):
        b, u, w, q = field[site], differ[site], image[site], image_two[site]
        residual[site] = u + kappa * w - sigma * q
        solved[site] = (1.0 - kappa) * b + sigma * u + dot(correction, vectors[site], NN)


def call(kernel, scalars, arrays, outs, name, cost=None):
    return pl.pallas_call(
        kernel,
        out_shape=[jax.ShapeDtypeStruct(shape, kind) for shape, kind in outs],
        in_specs=[pl.BlockSpec(memory_space=pltpu.SMEM)] * len(scalars)
        + [pl.BlockSpec(memory_space=pltpu.VMEM)] * len(arrays),
        out_specs=[pl.BlockSpec(memory_space=pltpu.VMEM)] * len(outs),
        compiler_params=pltpu.CompilerParams(vmem_limit_bytes=16 * 1024 * 1024),
        cost_estimate=cost,
        name=name,
    )(*scalars, *arrays)


def exchange(field, copies):
    outer = [lax.ppermute(field, axis, OUTER) for axis in (TA, XY, GZ)]
    near = lax.all_to_all(copies, BLOCK, 0, 0, tiled=True)
    return near.reshape(8, *field.shape), outer[0], outer[2], outer[1]


def body(right_side, stencil, restrict, aggregate, coarsest_inverse):
    field = right_side[0, 0, 0]
    vectors = restrict[0, 0, 0]
    local = (field.shape, F32)
    label = aggregate.reshape(2)
    (weights,) = call(
        prepare_kernel,
        (),
        (stencil[0, 0, 0],),
        (((2, 4, 256, 256), BF16),),
        "prepare",
        pl.CostEstimate(flops=1 << 20, bytes_accessed=1 << 23, transcendentals=0),
    )
    copies = jnp.broadcast_to(field[None], (8, *field.shape))
    image, differ, copies = call(
        first_kernel,
        (),
        (field, *exchange(field, copies), weights),
        (local, local, ((8, *field.shape), F32)),
        "first_image",
    )
    (early,) = call(
        early_kernel, (label,), (differ, image, vectors), (((32, 128), F32),), "early_part"
    )
    image_two, send = call(
        second_kernel,
        (),
        (differ, *exchange(differ, copies), weights, image, vectors, early),
        (local, ((8, 8, 128), F32)),
        "second_image",
    )
    recv = lax.all_to_all(send, BLOCK, 0, 0, tiled=True)
    (send,) = call(gather_kernel, (), (recv,), (((8, 8, 128), F32),), "block_sum")
    recv = lax.all_to_all(send.reshape(64, 128), LATTICE, 0, 0, tiled=True)
    send = pl.pallas_call(
        coarse_kernel,
        out_shape=jax.ShapeDtypeStruct((64, 128), F32),
        in_specs=[pl.BlockSpec(memory_space=pltpu.VMEM), pl.BlockSpec(memory_space=pltpu.HBM)],
        out_specs=pl.BlockSpec(memory_space=pltpu.VMEM),
        scratch_shapes=[pltpu.VMEM((128, 2048), F32), pltpu.SemaphoreType.DMA((2,))],
        compiler_params=pltpu.CompilerParams(vmem_limit_bytes=65900000),
        name="coarse_solve",
    )(recv, coarsest_inverse)
    recv = lax.all_to_all(send, LATTICE, 0, 0, tiled=True)
    (send,) = call(spread_kernel, (), (recv,), (((8, 8, 128), F32),), "block_spread")
    recv = lax.all_to_all(send, BLOCK, 0, 0, tiled=True)
    solved, residual = call(
        last_kernel,
        (),
        (recv, field, differ, image, image_two, vectors),
        (local, local),
        "last_update",
    )
    return solved[None, None, None], residual[None, None, None]


def solution(mesh):
    blocks = Mesh(mesh.devices.reshape(4, 2, 4, 2, 4, 2), ("T", "a", "Z", "b", "Y", "c"))
    spec = P(TA, GZ, XY)
    return jax.shard_map(
        body,
        mesh=blocks,
        in_specs=(spec, spec, spec, spec, P(XY)),
        out_specs=(spec, spec),
        check_vma=False,
    )
```

time: 112 us -> 109 us (0.973)
  blocking collectives: 26 us -> 58.6 us
  waiting for transfers between devices: 23.3 us -> 0.51 us
  starting transfers between devices: 49.6 us -> 39.5 us
  Pallas kernels: 8.24 us -> 6.19 us
    all_to_all x1 -> x4, blocking collectives: 26 us -> 58.6 us  [the longest x1 22.9 us: body(): recv = lax.all_to_all(send.reshape(64, 128), LATTICE, 0, 0, tiled=True)]
    all_to_all x1 -> x2, waiting for transfers between devices: 17.6 us -> 0.01 us  [exchange(): near = lax.all_to_all(copies, BLOCK, 0, 0, tiled=True)]
    ppermute x12 -> x6, starting transfers between devices: 37.6 us -> 24.2 us  [exchange(): outer = [lax.ppermute(field, axis, OUTER) for axis in (TA, XY, GZ)]]
    ppermute x12 -> x6, waiting for transfers between devices: 5.69 us -> 0.5 us  [exchange(): outer = [lax.ppermute(field, axis, OUTER) for axis in (TA, XY, GZ)]]
    all_to_all x1 -> x2, starting transfers between devices: 12 us -> 15.3 us  [exchange(): near = lax.all_to_all(copies, BLOCK, 0, 0, tiled=True)]
    unnamed x16 -> x8, local copies, waits for them, and re-layouts: 3.45 us -> 1.28 us
    pallas_call x4 -> x8, Pallas kernels: 8.24 us -> 6.19 us  [the longest x7 3.4 us: call(): pl.pallas_call(kernel, out_shape=[jax.ShapeDtypeStruct(shape, kind) for s...]
    broadcast_in_dim x0 -> x1, local copies, waits for them, and re-layouts: none -> 1.54 us  [body(): copies = jnp.broadcast_to(field[None], (8, *field.shape))]
  transfers between devices with their start and end apart: 13 -> 8, of which waited for: 4 -> 1; matrix products, arithmetic and copies ran while one was open for 0% -> 0% of each run, Pallas kernels for 0% -> 1%
where the time goes in v2:
time: 109 us; the launch traced here: 108 us
  blocking collectives  58.6 us (54%)
  starting transfers between devices  39.5 us (36%)
  Pallas kernels  6.19 us (6%)
  local copies, waits for them, and re-layouts  2.82 us (3%)
    ppermute x6, starting transfers between devices, exchange(): outer = [lax.ppermute(field, axis, OUTER) for axis in (TA, XY, GZ)]  24.2 us
    all_to_all x1, blocking collectives, body(): recv = lax.all_to_all(send.reshape(64, 128), LATTICE, 0, 0, tiled=True)  22.9 us
    all_to_all x2, blocking collectives, body(): recv = lax.all_to_all(send, BLOCK, 0, 0, tiled=True)  18 us
    all_to_all x1, blocking collectives, body(): recv = lax.all_to_all(send, LATTICE, 0, 0, tiled=True)  17.7 us
    all_to_all x2, starting transfers between devices, exchange(): near = lax.all_to_all(copies, BLOCK, 0, 0, tiled=True)  15.3 us
    pallas_call x7, Pallas kernels, call(): pl.pallas_call(kernel, out_shape=[jax.ShapeDtypeStruct(shape, kind) for s...  3.4 us
    pallas_call x1, Pallas kernels, body(): pl.pallas_call(coarse_kernel, out_shape=jax.ShapeDtypeStruct((64, 128), F...  2.8 us
  transfers between devices with their start and end apart: 8, of which 1 were waited for; matrix products, arithmetic and copies ran while one was open for 0% of the time, Pallas kernels for 1%

profile of v2, /device:TPU:1, one launch (start us, length us, event | category | flops | bytes accessed | tf_op | source)
XLA Modules:
  0.0 108.4 jit_solution(6616147935769779650)
XLA Ops:
  0.6 0.0 copy-start.1
  0.6 1.5 %broadcast_in_dim.11 = f32[8,2,32,128]{3,2,1,0:T(8,128)} broadcast(f32[2,32,128]{2,1,0:T(8,128)} %bitcast.15), dimensions={1,2,3} | broadcast | bytes 294912 | tf_op jit(solution)/shard_map/broadcast_in_dim | solution.py:237
  2.2 10.2 %all-to-all-start = ((f32[8,2,32,128]{3,2,1,0:T(8,128)}), f32[8,2,32,128]{3,2,1,0:T(8,128)S(1)}, u32[]{:S(2)}, u32[]{:S(2)}) async-start(f32[8,2,32,128]{3,2,1,0:T(8,128)} %broadcast_in_dim.11), calls=%async_computation | async-start | bytes 524288 | tf_op jit(solution)/shard_map/all_to_all | solution.py:220
  12.3 5.9 %collective-permute-start.2 = (f32[2,32,128]{2,1,0:T(8,128)}, f32[2,32,128]{2,1,0:T(8,128)S(1)}, u32[]{:S(2)}, u32[]{:S(2)}) collective-permute-start(f32[2,32,128]{2,1,0:T(8,128)} %bitcast.16), channel_id=1, source_target_pairs={{1,2},{2,1},{3,4},{4,3},{5,6},{6,5},{7,0},{0,7},{9,10},{10,9},{11,... | collective-permute-start | bytes 98312 | tf_op jit(solution)/shard_map/ppermute | solution.py:219
  18.3 3.7 %collective-permute-start.1 = (f32[2,32,128]{2,1,0:T(8,128)}, f32[2,32,128]{2,1,0:T(8,128)S(1)}, u32[]{:S(2)}, u32[]{:S(2)}) collective-permute-start(f32[2,32,128]{2,1,0:T(8,128)} %bitcast.17), channel_id=1, source_target_pairs={{8,16},{16,8},{24,32},{32,24},{40,48},{48,40},{56,0},{0,56},{9,17}... | collective-permute-start | bytes 98312 | tf_op jit(solution)/shard_map/ppermute | solution.py:219
  21.9 5.5 %collective-permute-start = (f32[2,32,128]{2,1,0:T(8,128)}, f32[2,32,128]{2,1,0:T(8,128)S(1)}, u32[]{:S(2)}, u32[]{:S(2)}) collective-permute-start(f32[2,32,128]{2,1,0:T(8,128)} %bitcast.18), channel_id=1, source_target_pairs={{64,128},{128,64},{192,256},{256,192},{320,384},{384,320},{448,0},... | collective-permute-start | bytes 98312 | tf_op jit(solution)/shard_map/ppermute | solution.py:219
  27.4 0.0 copy-start
  27.4 1.3 %copy-done = f32[1,1,1,2,9,128,128]{6,5,4,3,2,1,0:T(8,128)S(1)} copy-done((f32[1,1,1,2,9,128,128]{6,5,4,3,2,1,0:T(8,128)S(1)}, f32[1,1,1,2,9,128,128]{6,5,4,3,2,1,0:T(8,128)}, u32[]{:S(2)}) %copy-start) | copy-done | bytes 1179672
  28.7 0.0 copy-start.2
  28.7 0.0 copy-start.3
  28.7 0.3 prepare.1.weights
  29.0 0.0 collective-permute-done.2.o2
  29.1 0.0 collective-permute-done.1.o1
  29.1 0.0 collective-permute-done.o0
  29.1 0.0 all-to-all-done.near
  29.1 0.0 copy-done.1
  29.1 1.0 first_image.1
  30.1 5.1 %all-to-all-start.1 = ((f32[8,2,32,128]{3,2,1,0:T(8,128)}), f32[8,2,32,128]{3,2,1,0:T(8,128)S(1)}, u32[]{:S(2)}, u32[]{:S(2)}) async-start(f32[8,2,32,128]{3,2,1,0:T(8,128)} %get-tuple-element.10), calls=%async_computation.1 | async-start | bytes 524288 | tf_op jit(solution)/shard_map/all_to_all | solution.py:220
  35.2 2.3 %collective-permute-start.5 = (f32[2,32,128]{2,1,0:T(8,128)S(1)}, f32[2,32,128]{2,1,0:T(8,128)S(1)}, u32[]{:S(2)}, u32[]{:S(2)}) collective-permute-start(f32[2,32,128]{2,1,0:T(8,128)S(1)} %get-tuple-element.9.differ), channel_id=1, source_target_pairs={{1,2},{2,1},{3,4},{4,3},{5,6},{6,5},{7,0},{0,7},{9,10},{10,9},{11,... | collective-permute-start | bytes 98312 | tf_op jit(solution)/shard_map/ppermute | solution.py:219
  37.6 1.9 %collective-permute-start.4 = (f32[2,32,128]{2,1,0:T(8,128)S(1)}, f32[2,32,128]{2,1,0:T(8,128)S(1)}, u32[]{:S(2)}, u32[]{:S(2)}) collective-permute-start(f32[2,32,128]{2,1,0:T(8,128)S(1)} %get-tuple-element.9.differ), channel_id=1, source_target_pairs={{8,16},{16,8},{24,32},{32,24},{40,48},{48,40},{56,0},{0,56},{9,17}... | collective-permute-start | bytes 98312 | tf_op jit(solution)/shard_map/ppermute | solution.py:219
  39.5 4.9 %collective-permute-start.3 = (f32[2,32,128]{2,1,0:T(8,128)S(1)}, f32[2,32,128]{2,1,0:T(8,128)S(1)}, u32[]{:S(2)}, u32[]{:S(2)}) collective-permute-start(f32[2,32,128]{2,1,0:T(8,128)S(1)} %get-tuple-element.9.differ), channel_id=1, source_target_pairs={{64,128},{128,64},{192,256},{256,192},{320,384},{384,320},{448,0},... | collective-permute-start | bytes 98312 | tf_op jit(solution)/shard_map/ppermute | solution.py:219
  44.4 0.0 copy-done.2
  44.5 0.0 copy-done.3
  44.5 0.8 early_part.1.early
  45.2 0.0 collective-permute-done.5.o2
  45.2 0.0 collective-permute-done.4.o1
  45.2 0.5 collective-permute-done.3.o0
  45.7 0.0 all-to-all-done.1.near
  45.7 0.5 second_image.1
  46.2 8.5 %all_to_all.42.recv = f32[8,8,128]{2,1,0:T(8,128)S(1)} all-to-all(f32[8,8,128]{2,1,0:T(8,128)S(1)} %get-tuple-element.12), channel_id=1, replica_groups=mesh['T'=4,'a'=2,'Z'=4,'b'=2,'Y'=4,'c'=2] {'a','b','c'}, dimensions={0} | all-to-all | bytes 65536 | tf_op jit(solution)/shard_map/all_to_all | solution.py:255
  54.7 22.9 %all_to_all.43 = f32[64,1,128]{2,1,0:T(1,128)} all-to-all(f32[64,1,128]{2,1,0:T(1,128)S(1)} %bitcast.24), channel_id=1, replica_groups=mesh['T'=4,'a'=2,'Z'=4,'b'=2,'Y'=4,'c'=2] {'T','Z','Y'}, dimensions={0} | all-to-all | bytes 65536 | tf_op jit(solution)/shard_map/all_to_all | solution.py:257
  77.6 2.8 %coarse_solve.1 = f32[64,128]{1,0:T(8,128)} custom-call(f32[64,128]{1,0:T(8,128)} %bitcast.27, f32[256,2048]{1,0:T(8,128)} %inverse.1), custom_call_target="tpu_custom_call" | custom-call | tf_op jit(solution)/shard_map/coarse_solve/pallas_call | solution.py:258
  80.4 17.7 %all_to_all.44 = f32[64,1,128]{2,1,0:T(1,128)S(1)} all-to-all(f32[64,1,128]{2,1,0:T(1,128)} %bitcast.28), channel_id=1, replica_groups=mesh['T'=4,'a'=2,'Z'=4,'b'=2,'Y'=4,'c'=2] {'T','Z','Y'}, dimensions={0} | all-to-all | bytes 65536 | tf_op jit(solution)/shard_map/all_to_all | solution.py:267
  98.1 9.5 %all_to_all.45.recv = f32[8,8,128]{2,1,0:T(8,128)S(1)} all-to-all(f32[8,8,128]{2,1,0:T(8,128)S(1)} %block_spread.1), channel_id=1, replica_groups=mesh['T'=4,'a'=2,'Z'=4,'b'=2,'Y'=4,'c'=2] {'a','b','c'}, dimensions={0} | all-to-all | bytes 65536 | tf_op jit(solution)/shard_map/all_to_all | solution.py:269
  107.6 0.8 last_update.1
  (2 shorter events, 0.0 us)
Async XLA Ops:
  0.6 28.5 %copy-start.1 = (f32[1,1,1,2,32,128]{5,4,3,2,1,0:T(8,128)S(1)}, f32[1,1,1,2,32,128]{5,4,3,2,1,0:T(8,128)}, u32[]{:S(2)}) copy-start(f32[1,1,1,2,32,128]{5,4,3,2,1,0:T(8,128)} %param.5) | copy-start | bytes 98308
  2.2 26.9 %all-to-all-start = ((f32[8,2,32,128]{3,2,1,0:T(8,128)}), f32[8,2,32,128]{3,2,1,0:T(8,128)S(1)}, u32[]{:S(2)}, u32[]{:S(2)}) async-start(f32[8,2,32,128]{3,2,1,0:T(8,128)} %broadcast_in_dim.11), calls=%async_computation | async-start | bytes 524288 | tf_op jit(solution)/shard_map/all_to_all | solution.py:220
  12.3 16.7 %collective-permute-start.2 = (f32[2,32,128]{2,1,0:T(8,128)}, f32[2,32,128]{2,1,0:T(8,128)S(1)}, u32[]{:S(2)}, u32[]{:S(2)}) collective-permute-start(f32[2,32,128]{2,1,0:T(8,128)} %bitcast.16), channel_id=1, source_target_pairs={{1,2},{2,1},{3,4},{4,3},{5,6},{6,5},{7,0},{0,7},{9,10},{10,9},{11,... | collective-permute-start | bytes 98312 | tf_op jit(solution)/shard_map/ppermute | solution.py:219
  18.3 10.8 %collective-permute-start.1 = (f32[2,32,128]{2,1,0:T(8,128)}, f32[2,32,128]{2,1,0:T(8,128)S(1)}, u32[]{:S(2)}, u32[]{:S(2)}) collective-permute-start(f32[2,32,128]{2,1,0:T(8,128)} %bitcast.17), channel_id=1, source_target_pairs={{8,16},{16,8},{24,32},{32,24},{40,48},{48,40},{56,0},{0,56},{9,17}... | collective-permute-start | bytes 98312 | tf_op jit(solution)/shard_map/ppermute | solution.py:219
  21.9 7.1 %collective-permute-start = (f32[2,32,128]{2,1,0:T(8,128)}, f32[2,32,128]{2,1,0:T(8,128)S(1)}, u32[]{:S(2)}, u32[]{:S(2)}) collective-permute-start(f32[2,32,128]{2,1,0:T(8,128)} %bitcast.18), channel_id=1, source_target_pairs={{64,128},{128,64},{192,256},{256,192},{320,384},{384,320},{448,0},... | collective-permute-start | bytes 98312 | tf_op jit(solution)/shard_map/ppermute | solution.py:219
  27.4 1.3 %copy-start = (f32[1,1,1,2,9,128,128]{6,5,4,3,2,1,0:T(8,128)S(1)}, f32[1,1,1,2,9,128,128]{6,5,4,3,2,1,0:T(8,128)}, u32[]{:S(2)}) copy-start(f32[1,1,1,2,9,128,128]{6,5,4,3,2,1,0:T(8,128)} %param.6) | copy-start | bytes 3538948
  28.7 15.7 %copy-start.2 = (f32[1,1,1,2,32,128]{5,4,3,2,1,0:T(8,128)S(1)}, f32[1,1,1,2,32,128]{5,4,3,2,1,0:T(8,128)}, u32[]{:S(2)}) copy-start(f32[1,1,1,2,32,128]{5,4,3,2,1,0:T(8,128)} %param.7) | copy-start | bytes 98308
  28.7 15.8 %copy-start.3 = (s32[1,1,1,2]{3,2,1,0:T(1,128)S(1)}, s32[1,1,1,2]{3,2,1,0:T(1,128)}, u32[]{:S(2)}) copy-start(s32[1,1,1,2]{3,2,1,0:T(1,128)} %param.8) | copy-start | bytes 28
  30.1 15.6 %all-to-all-start.1 = ((f32[8,2,32,128]{3,2,1,0:T(8,128)}), f32[8,2,32,128]{3,2,1,0:T(8,128)S(1)}, u32[]{:S(2)}, u32[]{:S(2)}) async-start(f32[8,2,32,128]{3,2,1,0:T(8,128)} %get-tuple-element.10), calls=%async_computation.1 | async-start | bytes 524288 | tf_op jit(solution)/shard_map/all_to_all | solution.py:220
  35.2 10.0 %collective-permute-start.5 = (f32[2,32,128]{2,1,0:T(8,128)S(1)}, f32[2,32,128]{2,1,0:T(8,128)S(1)}, u32[]{:S(2)}, u32[]{:S(2)}) collective-permute-start(f32[2,32,128]{2,1,0:T(8,128)S(1)} %get-tuple-element.9.differ), channel_id=1, source_target_pairs={{1,2},{2,1},{3,4},{4,3},{5,6},{6,5},{7,0},{0,7},{9,10},{10,9},{11,... | collective-permute-start | bytes 98312 | tf_op jit(solution)/shard_map/ppermute | solution.py:219
  37.6 7.6 %collective-permute-start.4 = (f32[2,32,128]{2,1,0:T(8,128)S(1)}, f32[2,32,128]{2,1,0:T(8,128)S(1)}, u32[]{:S(2)}, u32[]{:S(2)}) collective-permute-start(f32[2,32,128]{2,1,0:T(8,128)S(1)} %get-tuple-element.9.differ), channel_id=1, source_target_pairs={{8,16},{16,8},{24,32},{32,24},{40,48},{48,40},{56,0},{0,56},{9,17}... | collective-permute-start | bytes 98312 | tf_op jit(solution)/shard_map/ppermute | solution.py:219
  39.5 6.2 %collective-permute-start.3 = (f32[2,32,128]{2,1,0:T(8,128)S(1)}, f32[2,32,128]{2,1,0:T(8,128)S(1)}, u32[]{:S(2)}, u32[]{:S(2)}) collective-permute-start(f32[2,32,128]{2,1,0:T(8,128)S(1)} %get-tuple-element.9.differ), channel_id=1, source_target_pairs={{64,128},{128,64},{192,256},{256,192},{320,384},{384,320},{448,0},... | collective-permute-start | bytes 98312 | tf_op jit(solution)/shard_map/ppermute | solution.py:219

commit v3 on v2

--- a/solution.py
+++ b/solution.py
@@ -123,77 +123,83 @@
             send[2 * group + c] = packed[8 * group : 8 * group + 8]
 
 
+def copy_kernel(field, send):
+    for other in range(8):
+        send[other] = field[...]
+
+
 def gather_kernel(recv, send):
     total = recv[0]
     for other in range(1, 8):
         total = total + recv[other]
-    for right in range(8):
-        send[right] = jnp.broadcast_to(total[right : right + 1], (8, 128))
+    for other in range(64):
+        send[other] = total
 
 
 def coarse_kernel(recv, inverse, send, rows_held, arrived):
-    half = lax.rem(lax.axis_index("Z"), 2)
     copies = []
     for part in range(2):
-        start = pl.multiple_of(128 * half + 64 * part, 64)
         copy = pltpu.make_async_copy(
-            inverse.at[pl.ds(start, 64)], rows_held.at[pl.ds(64 * part, 64)], arrived.at[part]
+            inverse.at[pl.ds(128 * part, 128)], rows_held.at[pl.ds(128 * part, 128)], arrived.at[part]
         )
         copy.start()
         copies.append(copy)
-    lane = lax.broadcasted_iota(jnp.int32, (1, 128), 1)
-    part = recv[...]
-    total = jnp.sum(part, axis=0, keepdims=True)
+    lane = lax.broadcasted_iota(jnp.int32, (8, 128), 1)
 
     def pick(row, place):
         return jnp.sum(jnp.where(lane == place, row, 0.0), axis=1, keepdims=True)
 
+    total = recv[0]
+    for source in range(1, 64):
+        total = total + recv[source]
     ww, wu, wq, qu, qq = [pick(total, 96 + place) for place in range(5)]
     first = wu / ww
     gamma = wq / ww
     sigma = (qu - gamma * wu) / (qq - gamma * wq)
     kappa = sigma * gamma - first
-    labels = pick(part, 101) * 0.125
-    mixed = part + kappa * pltpu.roll(part, 96, 1) - sigma * pltpu.roll(part, 64, 1)
-    mixed = jnp.where(lane < 32, mixed, 0.0)
-    mixed = mixed + pltpu.roll(mixed, 32, 1)
-    mixed = mixed + pltpu.roll(mixed, 64, 1)
     group = (lane // 32).astype(F32)
-    rows = []
-    for place in range(16):
-        chosen = labels == group + 4.0 * place
-        rows.append(jnp.sum(jnp.where(chosen, mixed, 0.0), axis=0, keepdims=True))
-    pieces = []
+    rows = [jnp.zeros((8, 128), F32) for _ in range(16)]
+    for source in range(64):
+        part = recv[source]
+        code = pick(part, 101) * 0.125 - group
+        mixed = part + kappa * pltpu.roll(part, 96, 1) - sigma * pltpu.roll(part, 64, 1)
+        mixed = jnp.where(lane < 32, mixed, 0.0)
+        mixed = mixed + pltpu.roll(mixed, 32, 1)
+        mixed = mixed + pltpu.roll(mixed, 64, 1)
+        for place in range(16):
+            rows[place] = rows[place] + jnp.where(code == 4.0 * place, mixed, 0.0)
+    high, low = split(jnp.concatenate(rows, axis=1))
+    both = jnp.concatenate([high, low], axis=0)
+    base = (8 * lax.axis_index(XY)).astype(F32)
+    own = 16 * lax.axis_index("T") + 4 * lax.axis_index("Z")
+    labels = [pick(recv[own + y], 101) * 0.125 - base for y in range(4)]
+    scalars = jnp.where(lane == 32, sigma, jnp.where(lane == 33, kappa, 0.0))
+    out = [jnp.zeros((8, 128), F32) for _ in range(4)]
     for part in range(2):
         copies[part].wait()
-        begin = 64 * part
-        piece = rows_held[begin : begin + 64, 0:128] * rows[0]
-        for place in range(1, 16):
-            piece = piece + rows_held[begin : begin + 64, 128 * place : 128 * place + 128] * rows[place]
-        pieces.append(piece)
-    solved = jnp.transpose(jnp.concatenate(pieces, axis=0))
-    solved = jnp.sum(solved, axis=0, keepdims=True)
-    scalars = jnp.where(lane == 32, sigma, jnp.where(lane == 33, kappa, 0.0))
-    base = (8 * lax.axis_index(XY) + 4 * half).astype(F32)
-    out = jnp.zeros((64, 128), F32)
-    for place in range(4):
-        row = pltpu.roll(solved, 128 - 32 * place, 1) if place else solved
-        row = jnp.where(lane < 32, row, scalars)
-        out = jnp.where(labels == base + float(place), row, out)
-    send[...] = out
-
-
-def spread_kernel(recv, send):
-    rows = []
-    for right in range(8):
-        rows.append(jnp.sum(recv[8 * right : 8 * right + 8], axis=0, keepdims=True))
-    value = jnp.concatenate(rows, axis=0)
-    for other in range(8):
-        send[other] = value
+        held_high, held_low = split(rows_held[128 * part : 128 * part + 128])
+        value = lax.dot_general(both, held_high, NT, preferred_element_type=F32)
+        value = value[0:8] + value[8:16]
+        value = value + lax.dot_general(high, held_low, NT, preferred_element_type=F32)
+        for place in range(4):
+            row = pltpu.roll(value, 128 - 32 * place, 1) if place else value
+            row = jnp.where(lane < 32, row, scalars)
+            for y in range(4):
+                out[y] = jnp.where(labels[y] == float(4 * part + place), row, out[y])
+    for side in range(4):
+        for y in range(4):
+            for c in range(2):
+                send[8 * side + 2 * y + c] = out[y]
 
 
 def last_kernel(recv, field, differ, image, image_two, vectors, solved, residual):
-    got = jnp.concatenate([recv[2 * group] + recv[2 * group + 1] for group in range(4)], axis=0)
+    groups = []
+    for group in range(4):
+        total = recv[8 * group]
+        for other in range(1, 8):
+            total = total + recv[8 * group + other]
+        groups.append(total)
+    got = jnp.concatenate(groups, axis=0)
     correction = got[:, 0:32]
     sigma, kappa = got[:, 32:33], got[:, 33:34]
     for site in range(2):
@@ -234,7 +240,7 @@
         "prepare",
         pl.CostEstimate(flops=1 << 20, bytes_accessed=1 << 23, transcendentals=0),
     )
-    copies = jnp.broadcast_to(field[None], (8, *field.shape))
+    (copies,) = call(copy_kernel, (), (field,), (((8, *field.shape), F32),), "copies")
     image, differ, copies = call(
         first_kernel,
         (),
@@ -253,20 +259,18 @@
         "second_image",
     )
     recv = lax.all_to_all(send, BLOCK, 0, 0, tiled=True)
-    (send,) = call(gather_kernel, (), (recv,), (((8, 8, 128), F32),), "block_sum")
-    recv = lax.all_to_all(send.reshape(64, 128), LATTICE, 0, 0, tiled=True)
+    (send,) = call(gather_kernel, (), (recv,), (((64, 8, 128), F32),), "block_sum")
+    recv = lax.all_to_all(send, LATTICE, 0, 0, tiled=True)
     send = pl.pallas_call(
         coarse_kernel,
-        out_shape=jax.ShapeDtypeStruct((64, 128), F32),
+        out_shape=jax.ShapeDtypeStruct((32, 8, 128), F32),
         in_specs=[pl.BlockSpec(memory_space=pltpu.VMEM), pl.BlockSpec(memory_space=pltpu.HBM)],
         out_specs=pl.BlockSpec(memory_space=pltpu.VMEM),
-        scratch_shapes=[pltpu.VMEM((128, 2048), F32), pltpu.SemaphoreType.DMA((2,))],
-        compiler_params=pltpu.CompilerParams(vmem_limit_bytes=65900000),
+        scratch_shapes=[pltpu.VMEM((256, 2048), F32), pltpu.SemaphoreType.DMA((2,))],
+        compiler_params=pltpu.CompilerParams(vmem_limit_bytes=65100000),
         name="coarse_solve",
     )(recv, coarsest_inverse)
-    recv = lax.all_to_all(send, LATTICE, 0, 0, tiled=True)
-    (send,) = call(spread_kernel, (), (recv,), (((8, 8, 128), F32),), "block_spread")
-    recv = lax.all_to_all(send, BLOCK, 0, 0, tiled=True)
+    recv = lax.all_to_all(send, ("a", "b", "Y", "c"), 0, 0, tiled=True)
     solved, residual = call(
         last_kernel,
         (),

time: 109 us -> 106 us (0.972)
  blocking collectives: 58.6 us -> 48.4 us
  Pallas kernels: 6.19 us -> 14.7 us
  local copies, waits for them, and re-layouts: 2.82 us -> 1.27 us
    all_to_all x2 -> x1, blocking collectives: 18 us -> 8.49 us  [body(): recv = lax.all_to_all(send, BLOCK, 0, 0, tiled=True)]
    all_to_all x1, blocking collectives: 22.9 us -> 14.5 us  [body(): recv = lax.all_to_all(send, ('a', 'b', 'Y', 'c'), 0, 0, tiled=True)]
    all_to_all x1, blocking collectives: 17.7 us -> 25.5 us  [body(): recv = lax.all_to_all(send, LATTICE, 0, 0, tiled=True)]
    pallas_call x1, Pallas kernels: 2.8 us -> 8.26 us  [body(): pl.pallas_call(coarse_kernel, out_shape=jax.ShapeDtypeStruct((32, 8, 128)...]
    pallas_call x7, Pallas kernels: 3.4 us -> 6.42 us  [call(): pl.pallas_call(kernel, out_shape=[jax.ShapeDtypeStruct(shape, kind) for s...]
    broadcast_in_dim x1 -> x0, local copies, waits for them, and re-layouts: 1.54 us -> none  [body(): copies = jnp.broadcast_to(field[None], (8, *field.shape))]
where the time goes in v3:
time: 106 us; the launch traced here: 105 us
  blocking collectives  48.4 us (46%)
  starting transfers between devices  39.5 us (37%)
  Pallas kernels  14.7 us (14%)
  local copies, waits for them, and re-layouts  1.27 us (1%)
    all_to_all x1, blocking collectives, body(): recv = lax.all_to_all(send, LATTICE, 0, 0, tiled=True)  25.5 us
    ppermute x6, starting transfers between devices, exchange(): outer = [lax.ppermute(field, axis, OUTER) for axis in (TA, XY, GZ)]  24.2 us
    all_to_all x2, starting transfers between devices, exchange(): near = lax.all_to_all(copies, BLOCK, 0, 0, tiled=True)  15.3 us
    all_to_all x1, blocking collectives, body(): recv = lax.all_to_all(send, ('a', 'b', 'Y', 'c'), 0, 0, tiled=True)  14.5 us
    all_to_all x1, blocking collectives, body(): recv = lax.all_to_all(send, BLOCK, 0, 0, tiled=True)  8.49 us
    pallas_call x1, Pallas kernels, body(): pl.pallas_call(coarse_kernel, out_shape=jax.ShapeDtypeStruct((32, 8, 128)...  8.26 us
    pallas_call x7, Pallas kernels, call(): pl.pallas_call(kernel, out_shape=[jax.ShapeDtypeStruct(shape, kind) for s...  6.42 us
  transfers between devices with their start and end apart: 8, of which 1 were waited for; matrix products, arithmetic and copies ran while one was open for 0% of the time, Pallas kernels for 1%

profile of v3, /device:TPU:1, one launch (start us, length us, event | category | flops | bytes accessed | tf_op | source)
XLA Modules:
  0.0 105.2 jit_solution(7260823524907175790)
XLA Ops:
  0.6 1.5 %copies.1 = f32[8,2,32,128]{3,2,1,0:T(8,128)} custom-call(f32[2,32,128]{2,1,0:T(8,128)} %bitcast.field), custom_call_target="tpu_custom_call" | custom-call | tf_op jit(solution)/shard_map/copies/pallas_call | solution.py:212
  2.1 10.2 %all-to-all-start = ((f32[8,2,32,128]{3,2,1,0:T(8,128)}), f32[8,2,32,128]{3,2,1,0:T(8,128)S(1)}, u32[]{:S(2)}, u32[]{:S(2)}) async-start(f32[8,2,32,128]{3,2,1,0:T(8,128)} %copies.1), calls=%async_computation | async-start | bytes 524288 | tf_op jit(solution)/shard_map/all_to_all | solution.py:226
  12.3 5.9 %collective-permute-start.2 = (f32[2,32,128]{2,1,0:T(8,128)}, f32[2,32,128]{2,1,0:T(8,128)S(1)}, u32[]{:S(2)}, u32[]{:S(2)}) collective-permute-start(f32[2,32,128]{2,1,0:T(8,128)} %bitcast.field), channel_id=1, source_target_pairs={{1,2},{2,1},{3,4},{4,3},{5,6},{6,5},{7,0},{0,7},{9,10},{10,9},{11,... | collective-permute-start | bytes 98312 | tf_op jit(solution)/shard_map/ppermute | solution.py:225
  18.2 3.7 %collective-permute-start.1 = (f32[2,32,128]{2,1,0:T(8,128)}, f32[2,32,128]{2,1,0:T(8,128)S(1)}, u32[]{:S(2)}, u32[]{:S(2)}) collective-permute-start(f32[2,32,128]{2,1,0:T(8,128)} %bitcast.field), channel_id=1, source_target_pairs={{8,16},{16,8},{24,32},{32,24},{40,48},{48,40},{56,0},{0,56},{9,17}... | collective-permute-start | bytes 98312 | tf_op jit(solution)/shard_map/ppermute | solution.py:225
  21.9 5.5 %collective-permute-start = (f32[2,32,128]{2,1,0:T(8,128)}, f32[2,32,128]{2,1,0:T(8,128)S(1)}, u32[]{:S(2)}, u32[]{:S(2)}) collective-permute-start(f32[2,32,128]{2,1,0:T(8,128)} %bitcast.field), channel_id=1, source_target_pairs={{64,128},{128,64},{192,256},{256,192},{320,384},{384,320},{448,0},... | collective-permute-start | bytes 98312 | tf_op jit(solution)/shard_map/ppermute | solution.py:225
  27.3 0.0 copy-start
  27.4 1.3 %copy-done = f32[1,1,1,2,9,128,128]{6,5,4,3,2,1,0:T(8,128)S(1)} copy-done((f32[1,1,1,2,9,128,128]{6,5,4,3,2,1,0:T(8,128)S(1)}, f32[1,1,1,2,9,128,128]{6,5,4,3,2,1,0:T(8,128)}, u32[]{:S(2)}) %copy-start) | copy-done | bytes 1179672
  28.6 0.0 copy-start.1
  28.6 0.0 copy-start.2
  28.6 0.3 prepare.1.weights
  29.0 0.0 collective-permute-done.2.o2
  29.0 0.0 collective-permute-done.1.o1
  29.0 0.0 collective-permute-done.o0
  29.0 0.0 all-to-all-done.near
  29.0 1.8 %first_image.1 = (f32[2,32,128]{2,1,0:T(8,128)S(1)}, f32[2,32,128]{2,1,0:T(8,128)S(1)}, f32[8,2,32,128]{3,2,1,0:T(8,128)}) custom-call(f32[2,32,128]{2,1,0:T(8,128)} %bitcast.field, f32[8,2,32,128]{3,2,1,0:T(8,128)S(1)} %all-to-all-done.near, f32[2,32,128]{2,1,0:T(8,128)S(1)} %collective-permute-done.o0, f32[2,32,128]{2,1,0:T(8,128)S(1)} %collective-permute-done.1.o1, ...), custom_call_target="tpu_custom_call" | custom-call | tf_op jit(solution)/shard_map/first_image/pallas_call | solution.py:212
  30.8 5.1 %all-to-all-start.1 = ((f32[8,2,32,128]{3,2,1,0:T(8,128)}), f32[8,2,32,128]{3,2,1,0:T(8,128)S(1)}, u32[]{:S(2)}, u32[]{:S(2)}) async-start(f32[8,2,32,128]{3,2,1,0:T(8,128)} %get-tuple-element.10), calls=%async_computation.1 | async-start | bytes 524288 | tf_op jit(solution)/shard_map/all_to_all | solution.py:226
  35.9 2.3 %collective-permute-start.5 = (f32[2,32,128]{2,1,0:T(8,128)S(1)}, f32[2,32,128]{2,1,0:T(8,128)S(1)}, u32[]{:S(2)}, u32[]{:S(2)}) collective-permute-start(f32[2,32,128]{2,1,0:T(8,128)S(1)} %get-tuple-element.9.differ), channel_id=1, source_target_pairs={{1,2},{2,1},{3,4},{4,3},{5,6},{6,5},{7,0},{0,7},{9,10},{10,9},{11,... | collective-permute-start | bytes 98312 | tf_op jit(solution)/shard_map/ppermute | solution.py:225
  38.3 1.9 %collective-permute-start.4 = (f32[2,32,128]{2,1,0:T(8,128)S(1)}, f32[2,32,128]{2,1,0:T(8,128)S(1)}, u32[]{:S(2)}, u32[]{:S(2)}) collective-permute-start(f32[2,32,128]{2,1,0:T(8,128)S(1)} %get-tuple-element.9.differ), channel_id=1, source_target_pairs={{8,16},{16,8},{24,32},{32,24},{40,48},{48,40},{56,0},{0,56},{9,17}... | collective-permute-start | bytes 98312 | tf_op jit(solution)/shard_map/ppermute | solution.py:225
  40.2 4.9 %collective-permute-start.3 = (f32[2,32,128]{2,1,0:T(8,128)S(1)}, f32[2,32,128]{2,1,0:T(8,128)S(1)}, u32[]{:S(2)}, u32[]{:S(2)}) collective-permute-start(f32[2,32,128]{2,1,0:T(8,128)S(1)} %get-tuple-element.9.differ), channel_id=1, source_target_pairs={{64,128},{128,64},{192,256},{256,192},{320,384},{384,320},{448,0},... | collective-permute-start | bytes 98312 | tf_op jit(solution)/shard_map/ppermute | solution.py:225
  45.1 0.0 copy-done.1
  45.1 0.0 copy-done.2
  45.2 0.8 early_part.1.early
  45.9 0.0 collective-permute-done.5.o2
  45.9 0.0 collective-permute-done.4.o1
  45.9 0.5 collective-permute-done.3.o0
  46.4 0.0 all-to-all-done.1.near
  46.4 0.5 second_image.1
  46.9 8.5 %all_to_all.25.recv = f32[8,8,128]{2,1,0:T(8,128)S(1)} all-to-all(f32[8,8,128]{2,1,0:T(8,128)S(1)} %get-tuple-element.12), channel_id=1, replica_groups=mesh['T'=4,'a'=2,'Z'=4,'b'=2,'Y'=4,'c'=2] {'a','b','c'}, dimensions={0} | all-to-all | bytes 65536 | tf_op jit(solution)/shard_map/all_to_all | solution.py:261
  55.4 25.5 %all_to_all.26.recv = f32[64,8,128]{2,1,0:T(8,128)} all-to-all(f32[64,8,128]{2,1,0:T(8,128)S(1)} %block_sum.1), channel_id=1, replica_groups=mesh['T'=4,'a'=2,'Z'=4,'b'=2,'Y'=4,'c'=2] {'T','Z','Y'}, dimensions={0} | all-to-all | bytes 524288 | tf_op jit(solution)/shard_map/all_to_all | solution.py:263
  80.9 8.3 %coarse_solve.1 = f32[32,8,128]{2,1,0:T(8,128)} custom-call(f32[64,8,128]{2,1,0:T(8,128)} %all_to_all.26.recv, f32[256,2048]{1,0:T(8,128)} %inverse.1), custom_call_target="tpu_custom_call" | custom-call | tf_op jit(solution)/shard_map/coarse_solve/pallas_call | solution.py:264
  89.2 14.5 %all_to_all.27.recv = f32[32,8,128]{2,1,0:T(8,128)S(1)} all-to-all(f32[32,8,128]{2,1,0:T(8,128)} %coarse_solve.1), channel_id=1, replica_groups=mesh['T'=4,'a'=2,'Z'=4,'b'=2,'Y'=4,'c'=2] {'a','b','Y','c'}, dimensions={0} | all-to-all | bytes 262144 | tf_op jit(solution)/shard_map/all_to_all | solution.py:273
  103.7 1.6 %last_update.1 = (f32[2,32,128]{2,1,0:T(8,128)}, f32[2,32,128]{2,1,0:T(8,128)}) custom-call(f32[32,8,128]{2,1,0:T(8,128)S(1)} %all_to_all.27.recv, f32[2,32,128]{2,1,0:T(8,128)} %bitcast.field, f32[2,32,128]{2,1,0:T(8,128)S(1)} %get-tuple-element.9.differ, f32[2,32,128]{2,1,0:T(8,128)S(1)} %get-tuple-element.11.image, ...), custom_call_target="tpu_custom_call" | custom-call | tf_op jit(solution)/shard_map/last_update/pallas_call | solution.py:212
  (1 shorter events, 0.0 us)
Async XLA Ops:
  2.1 26.9 %all-to-all-start = ((f32[8,2,32,128]{3,2,1,0:T(8,128)}), f32[8,2,32,128]{3,2,1,0:T(8,128)S(1)}, u32[]{:S(2)}, u32[]{:S(2)}) async-start(f32[8,2,32,128]{3,2,1,0:T(8,128)} %copies.1), calls=%async_computation | async-start | bytes 524288 | tf_op jit(solution)/shard_map/all_to_all | solution.py:226
  12.3 16.7 %collective-permute-start.2 = (f32[2,32,128]{2,1,0:T(8,128)}, f32[2,32,128]{2,1,0:T(8,128)S(1)}, u32[]{:S(2)}, u32[]{:S(2)}) collective-permute-start(f32[2,32,128]{2,1,0:T(8,128)} %bitcast.field), channel_id=1, source_target_pairs={{1,2},{2,1},{3,4},{4,3},{5,6},{6,5},{7,0},{0,7},{9,10},{10,9},{11,... | collective-permute-start | bytes 98312 | tf_op jit(solution)/shard_map/ppermute | solution.py:225
  18.2 10.8 %collective-permute-start.1 = (f32[2,32,128]{2,1,0:T(8,128)}, f32[2,32,128]{2,1,0:T(8,128)S(1)}, u32[]{:S(2)}, u32[]{:S(2)}) collective-permute-start(f32[2,32,128]{2,1,0:T(8,128)} %bitcast.field), channel_id=1, source_target_pairs={{8,16},{16,8},{24,32},{32,24},{40,48},{48,40},{56,0},{0,56},{9,17}... | collective-permute-start | bytes 98312 | tf_op jit(solution)/shard_map/ppermute | solution.py:225
  21.9 7.1 %collective-permute-start = (f32[2,32,128]{2,1,0:T(8,128)}, f32[2,32,128]{2,1,0:T(8,128)S(1)}, u32[]{:S(2)}, u32[]{:S(2)}) collective-permute-start(f32[2,32,128]{2,1,0:T(8,128)} %bitcast.field), channel_id=1, source_target_pairs={{64,128},{128,64},{192,256},{256,192},{320,384},{384,320},{448,0},... | collective-permute-start | bytes 98312 | tf_op jit(solution)/shard_map/ppermute | solution.py:225
  27.3 1.3 %copy-start = (f32[1,1,1,2,9,128,128]{6,5,4,3,2,1,0:T(8,128)S(1)}, f32[1,1,1,2,9,128,128]{6,5,4,3,2,1,0:T(8,128)}, u32[]{:S(2)}) copy-start(f32[1,1,1,2,9,128,128]{6,5,4,3,2,1,0:T(8,128)} %param.6) | copy-start | bytes 3538948
  28.6 16.5 %copy-start.1 = (f32[1,1,1,2,32,128]{5,4,3,2,1,0:T(8,128)S(1)}, f32[1,1,1,2,32,128]{5,4,3,2,1,0:T(8,128)}, u32[]{:S(2)}) copy-start(f32[1,1,1,2,32,128]{5,4,3,2,1,0:T(8,128)} %param.7) | copy-start | bytes 98308
  28.6 16.5 %copy-start.2 = (s32[1,1,1,2]{3,2,1,0:T(1,128)S(1)}, s32[1,1,1,2]{3,2,1,0:T(1,128)}, u32[]{:S(2)}) copy-start(s32[1,1,1,2]{3,2,1,0:T(1,128)} %param.8) | copy-start | bytes 28
  30.8 15.6 %all-to-all-start.1 = ((f32[8,2,32,128]{3,2,1,0:T(8,128)}), f32[8,2,32,128]{3,2,1,0:T(8,128)S(1)}, u32[]{:S(2)}, u32[]{:S(2)}) async-start(f32[8,2,32,128]{3,2,1,0:T(8,128)} %get-tuple-element.10), calls=%async_computation.1 | async-start | bytes 524288 | tf_op jit(solution)/shard_map/all_to_all | solution.py:226
  35.9 10.0 %collective-permute-start.5 = (f32[2,32,128]{2,1,0:T(8,128)S(1)}, f32[2,32,128]{2,1,0:T(8,128)S(1)}, u32[]{:S(2)}, u32[]{:S(2)}) collective-permute-start(f32[2,32,128]{2,1,0:T(8,128)S(1)} %get-tuple-element.9.differ), channel_id=1, source_target_pairs={{1,2},{2,1},{3,4},{4,3},{5,6},{6,5},{7,0},{0,7},{9,10},{10,9},{11,... | collective-permute-start | bytes 98312 | tf_op jit(solution)/shard_map/ppermute | solution.py:225
  38.3 7.6 %collective-permute-start.4 = (f32[2,32,128]{2,1,0:T(8,128)S(1)}, f32[2,32,128]{2,1,0:T(8,128)S(1)}, u32[]{:S(2)}, u32[]{:S(2)}) collective-permute-start(f32[2,32,128]{2,1,0:T(8,128)S(1)} %get-tuple-element.9.differ), channel_id=1, source_target_pairs={{8,16},{16,8},{24,32},{32,24},{40,48},{48,40},{56,0},{0,56},{9,17}... | collective-permute-start | bytes 98312 | tf_op jit(solution)/shard_map/ppermute | solution.py:225
  40.2 6.2 %collective-permute-start.3 = (f32[2,32,128]{2,1,0:T(8,128)S(1)}, f32[2,32,128]{2,1,0:T(8,128)S(1)}, u32[]{:S(2)}, u32[]{:S(2)}) collective-permute-start(f32[2,32,128]{2,1,0:T(8,128)S(1)} %get-tuple-element.9.differ), channel_id=1, source_target_pairs={{64,128},{128,64},{192,256},{256,192},{320,384},{384,320},{448,0},... | collective-permute-start | bytes 98312 | tf_op jit(solution)/shard_map/ppermute | solution.py:225
